TPU v7x, 512 devices: a whole 4x4x16 slice. The times are simulated.
512 devices in a mesh: dp: 8 (over y_hi, x), tile: 64 (over y_lo, z, core).
Axes of the slice: x: 4, y: 4 (y_hi: 2, y_lo: 2; y = y_hi * 2 + y_lo), z: 16, core: 2. Of those that a mesh axis runs over, the one named last changes fastest.
Arguments:
- ocean_state: bfloat16 [8, 256, 64, 768], P('dp', 'tile'), may hold values from -6 to 6
- cotangent: bfloat16 [8, 256, 64, 768], P('dp', 'tile'), may hold values from -6 to 6
- depth_kernel: float32 [7, 7, 768], replicated, may hold values from -0.875 to 0.875
- norm_gain: float32 [768], replicated, may hold values from 0.5 to 2
- expand_weight: bfloat16 [768, 3072], P('tile'), may hold values from -0.21875 to 0.21875
- expand_bias: float32 [3072], replicated, may hold values from -4 to 4
- reduce_weight: bfloat16 [3072, 768], P('tile'), may hold values from -0.109375 to 0.109375
- tile_slot: int32 [256], P('tile'), may hold values from -1 to 5, as said below
Outputs:
- state_grad: bfloat16 [8, 256, 64, 768], P('dp', 'tile')
- kernel_grad: float32 [7, 7, 768], replicated
- gain_grad: float32 [768], replicated
- bias_grad: float32 [3072], replicated
Inputs may be any that keep to these rules, and one draw needn't show every extreme that they name: `tile_slot`: entry t is -1 for a land tile, k < 3 for slot k of the tile's own device, 3 + k for slot k of the device whose tile index differs by half of the axis; the tiles of a device and of that device together name each slot of either at most once, and on some pair of devices every slot is named.
All inputs are finite; a program needn't handle non-finite values.
Results may differ from a plain program's by a relative error of at most 0.0085.
Values may be sent and summed in bfloat16 or wider, within the bound.
No kernel may reach another device: no remote copies, remote signals or barrier semaphores. Data moves between devices by JAX's collectives and lax.ppermute only.
A program may use at most 64 MiB of HBM per device.

v0:
```python
import math

import jax
import jax.numpy as jnp
from jax import lax
from jax.experimental import pallas as pl
from jax.experimental.pallas import tpu as pltpu
from jax.sharding import Mesh
from jax.sharding import PartitionSpec as P

KS = 7
TILE = ("yl", "z", "c")
DP = ("yh", "x")
PLANE = ("yh", "x", "yl", "c")


def with_halo(cells, width):
    count = lax.axis_size(TILE)
    ends = count - 1
    head = lax.slice_in_dim(cells, 0, width, axis=1)
    tail = lax.slice_in_dim(cells, cells.shape[1] - width, cells.shape[1], axis=1)
    return jnp.concatenate(
        [
            lax.ppermute(tail, TILE, [(i, i + 1) for i in range(ends)]),
            cells,
            lax.ppermute(head, TILE, [(i + 1, i) for i in range(ends)]),
        ],
        axis=1,
    )


def depthwise(padded, kernel, row_count, col_count):
    total = None
    for shift_row in range(KS):
        band = padded[..., shift_row : shift_row + row_count, :, :]
        part = kernel[shift_row, 0] * band[..., 0:col_count, :].astype(jnp.float32)
        for shift_col in range(1, KS):
            part = part + kernel[shift_row, shift_col] * band[
                ..., shift_col : shift_col + col_count, :
            ].astype(jnp.float32)
        total = part if total is None else total + part
    return total


def gelu_slope(value):
    factor = math.sqrt(2.0 / math.pi)
    inner = factor * (value + 0.044715 * value * value * value)
    tangent = jnp.tanh(inner)
    return 0.5 * (1.0 + tangent) + 0.5 * value * (1.0 - tangent * tangent) * factor * (
        1.0 + 3.0 * 0.044715 * value * value
    )


def sum_everywhere(parts):
    lanes = 128
    plane = lax.axis_size(PLANE)
    depth = lax.axis_size("z")
    rows = [part.reshape(-1, lanes) for part in parts]
    used = sum(piece.shape[0] for piece in rows)
    share = -(-used // (8 * plane)) * 8
    rows.append(jnp.zeros((share * plane - used, lanes), jnp.float32))
    stacked = jnp.concatenate(rows).reshape(plane, share, lanes)
    mine = jnp.sum(lax.all_to_all(stacked, PLANE, 0, 0), axis=0)
    mine = jnp.broadcast_to(mine[None], (depth, share, lanes))
    mine = jnp.sum(lax.all_to_all(mine, "z", 0, 0), axis=0)
    mine = jnp.broadcast_to(mine[None], (plane, share, lanes))
    full = lax.all_to_all(mine, PLANE, 0, 0).reshape(plane * share, lanes)
    out, start = [], 0
    for part in parts:
        count = part.size // lanes
        out.append(full[start : start + count].reshape(part.shape))
        start += count
    return out


NEAR = ((0, 1), (1, 0), (2, 3), (3, 2))
FAR = ((0, 3), (3, 0), (1, 2), (2, 1))
HIGH, WIDE = 24, 384


def column_of_weights(expand_weight, reduce_weight):
    core, column = lax.axis_index("c"), lax.axis_index("x")
    pair, side = column // 2, column % 2
    thin, units = expand_weight.shape
    part = lax.dynamic_slice(expand_weight, (0, side * (units // 2)), (thin, units // 2))
    row = lax.broadcasted_iota(jnp.int32, (units // 2, 2 * WIDE), 0)
    col = lax.broadcasted_iota(jnp.int32, (units // 2, 2 * WIDE), 1)
    band = col // WIDE * 2 + pair
    at = col % WIDE
    pick = row == at // HIGH * (4 * HIGH) + at % HIGH + band * HIGH
    chosen = jnp.dot(part, pick.astype(jnp.bfloat16), preferred_element_type=jnp.float32)
    both = lax.all_gather(chosen.astype(jnp.bfloat16), "c", axis=0)
    piece = jnp.where(
        lax.axis_index("yh") == 0,
        lax.dynamic_slice(both, (0, 0, core * WIDE), (2, thin, WIDE)).reshape(HIGH, WIDE),
        lax.dynamic_slice(reduce_weight, (pair * HIGH, side * WIDE), (HIGH, WIDE)),
    )
    depth = lax.axis_size("z")
    return lax.all_to_all(jnp.broadcast_to(piece[None], (depth, HIGH, WIDE)), "z", 0, 0)


def sheets_of_weights(column):
    depth = column.shape[0]
    own = lax.all_to_all(
        jnp.broadcast_to(column[None], (4, depth, HIGH, WIDE)), ("yh", "yl"), 0, 0
    ).reshape(2, 2 * depth * HIGH, WIDE)
    own_expand, own_reduce = own[0], own[1]
    near_expand = lax.ppermute(own_expand, "x", NEAR)
    far_reduce = lax.ppermute(own_reduce, "x", FAR)
    near_reduce = lax.ppermute(own_reduce, "x", NEAR)
    far_expand = lax.ppermute(own_expand, "x", FAR)
    across_expand = lax.ppermute(near_expand, "x", FAR)
    across_reduce = lax.ppermute(far_reduce, "x", NEAR)
    return (own_expand, near_expand, own_reduce, near_reduce), (
        far_expand,
        across_expand,
        far_reduce,
        across_reduce,
    )


def add_band(band, first_side, scaled_ref, masked_ref, bias_ref, sheets, bias_out, expand, reduce, sem, total):
    wide = expand.shape[2]
    contract_last = (((1,), (1,)), ((), ()))
    copies = [
        pltpu.make_async_copy(sheets[0], expand.at[0], sem.at[0]),
        pltpu.make_async_copy(sheets[2], reduce.at[0], sem.at[2]),
        pltpu.make_async_copy(sheets[3], reduce.at[1], sem.at[3]),
        pltpu.make_async_copy(sheets[1], expand.at[1], sem.at[1]),
    ]
    for copy in copies:
        copy.start()
    sides = (first_side, 1 - first_side)
    for part in range(2):
        half = pl.ds(pl.multiple_of(sides[part] * wide, wide), wide)
        copies[3 if part else 0].wait()
        hidden = jnp.dot(scaled_ref[...], expand[part], preferred_element_type=jnp.float32)
        slope = gelu_slope(hidden + bias_ref[band * 2 + sides[part]])
        back_act = None
        for other in range(2):
            if part == 0:
                copies[1 + other].wait()
            term = lax.dot_general(
                masked_ref[:, pl.ds(pl.multiple_of(sides[other] * wide, wide), wide)],
                reduce[other, half, :],
                contract_last,
                preferred_element_type=jnp.float32,
            )
            back_act = term if back_act is None else back_act + term
        back_hidden = (back_act * slope).astype(jnp.bfloat16)
        bias_out[band * 2 + sides[part]] = jnp.sum(back_hidden.astype(jnp.float32), axis=0, keepdims=True)
        total[...] += lax.dot_general(
            back_hidden, expand[part], contract_last, preferred_element_type=jnp.float32
        )


def first_body(
    where_ref, scaled_ref, masked_ref, bias_ref, s0, s1, s2, s3, total_ref, bias_out, expand, reduce, sem
):
    column, core = where_ref[0], where_ref[1]
    bias_out[...] = jnp.zeros_like(bias_out)
    total_ref[...] = jnp.zeros_like(total_ref)
    add_band(
        2 * core + lax.div(column, 2), lax.rem(column, 2), scaled_ref, masked_ref, bias_ref,
        (s0, s1, s2, s3), bias_out, expand, reduce, sem, total_ref,
    )


def second_body(
    where_ref, scaled_ref, masked_ref, bias_ref, s0, s1, s2, s3, sum_ref, bias_in,
    mine_ref, other_ref, bias_out, expand, reduce, total, sem,
):
    column, core = where_ref[0], where_ref[1]
    cells = mine_ref.shape[0]
    bias_out[...] = bias_in[...]
    total[...] = sum_ref[...]
    add_band(
        2 * core + 1 - lax.div(column, 2), 1 - lax.rem(column, 2), scaled_ref, masked_ref, bias_ref,
        (s0, s1, s2, s3), bias_out, expand, reduce, sem, total,
    )
    mine_ref[...] = total[pl.ds(pl.multiple_of(core * cells, cells), cells), :]
    other_ref[...] = total[pl.ds(pl.multiple_of((1 - core) * cells, cells), cells), :]


def norm_body(mine_ref, other_ref, normed_ref, inverse_ref, gain_ref, mixed_ref, gain_part_ref):
    gain_part_ref[...] = jnp.zeros_like(gain_part_ref)
    rows = 32

    def finish(step, carry):
        at = pl.ds(pl.multiple_of(step * rows, rows), rows)
        back = (mine_ref[at, :] + other_ref[at, :]).astype(jnp.bfloat16).astype(jnp.float32)
        normed = normed_ref[at, :]
        gain_part_ref[...] += jnp.sum(back * normed, axis=0, keepdims=True)
        back_norm = back * gain_ref[...]
        mixed = inverse_ref[at, :] * (
            back_norm
            - jnp.mean(back_norm, axis=-1, keepdims=True)
            - normed * jnp.mean(back_norm * normed, axis=-1, keepdims=True)
        )
        mixed_ref[at, :] = mixed.astype(jnp.bfloat16)
        return carry

    lax.fori_loop(0, mine_ref.shape[0] // rows, finish, 0)


def pointwise(where, scaled, masked, normed, inverse, gain, bias, first, second):
    cells, channels = normed.shape
    vmem = pl.BlockSpec(memory_space=pltpu.VMEM)
    there = pl.BlockSpec(memory_space=pl.ANY)
    smem = pl.BlockSpec(memory_space=pltpu.SMEM)
    weights = [pltpu.VMEM((2, channels, WIDE), jnp.bfloat16) for _ in range(2)]
    sem = pltpu.SemaphoreType.DMA((4,))
    whole = jax.ShapeDtypeStruct((2 * cells, channels), jnp.float32)
    half = jax.ShapeDtypeStruct((cells, channels), jnp.float32)
    bias_shape = jax.ShapeDtypeStruct(bias.shape, jnp.float32)
    params = pltpu.CompilerParams(vmem_limit_bytes=32 * 1024 * 1024)
    cost = pl.CostEstimate(
        flops=12 * cells * channels * channels, transcendentals=2 * cells * channels, bytes_accessed=20 * 1024 * 1024
    )
    total, bias_part = pl.pallas_call(
        first_body,
        out_shape=(whole, bias_shape),
        in_specs=[smem] + [vmem] * 3 + [there] * 4,
        out_specs=(vmem, vmem),
        scratch_shapes=weights + [sem],
        compiler_params=params,
        cost_estimate=cost,
        name="pointwise_first",
    )(where, scaled, masked, bias, *first)
    mine, other, bias_part = pl.pallas_call(
        second_body,
        out_shape=(half, half, bias_shape),
        in_specs=[smem] + [vmem] * 3 + [there] * 4 + [vmem] * 2,
        out_specs=(vmem, vmem, vmem),
        scratch_shapes=weights + [pltpu.VMEM((2 * cells, channels), jnp.float32), sem],
        compiler_params=params,
        cost_estimate=cost,
        name="pointwise_second",
    )(where, scaled, masked, bias, *second, total, bias_part)
    other = lax.ppermute(other, "c", ((0, 1), (1, 0)))
    mixed, gain_part = pl.pallas_call(
        norm_body,
        out_shape=(
            jax.ShapeDtypeStruct((cells, channels), jnp.bfloat16),
            jax.ShapeDtypeStruct((1, channels), jnp.float32),
        ),
        in_specs=[vmem] * 5,
        out_specs=(vmem, vmem),
        compiler_params=params,
        name="norm_back",
    )(mine, other, normed, inverse, gain)
    return mixed, gain_part, bias_part


def local(
    ocean_state,
    cotangent,
    depth_kernel,
    norm_gain,
    expand_weight,
    expand_bias,
    reduce_weight,
    tile_slot,
):
    samples, row_count, col_count, channels = ocean_state.shape
    tile_count = tile_slot.shape[0]
    tile_rows = row_count // tile_count
    rim = KS // 2
    weights_column = column_of_weights(expand_weight, reduce_weight)
    padded = with_halo(ocean_state, rim)
    padded = jnp.pad(padded, ((0, 0), (0, 0), (rim, rim), (0, 0)))
    mixed = depthwise(padded, depth_kernel, row_count, col_count)
    centred = mixed - jnp.mean(mixed, axis=-1, keepdims=True)
    inverse = lax.rsqrt(jnp.mean(centred * centred, axis=-1, keepdims=True) + 1e-06)
    normed = centred * inverse
    scaled = (normed * norm_gain).astype(jnp.bfloat16)
    row_mask = jnp.repeat(tile_slot >= 0, tile_rows).astype(jnp.bfloat16)
    masked = cotangent * row_mask[None, :, None, None]
    where = jnp.stack([lax.axis_index("x"), lax.axis_index("c")]).astype(jnp.int32)
    depth = lax.axis_size("z")
    ready = (
        scaled.reshape(-1, channels),
        masked.reshape(-1, channels),
        normed.reshape(-1, channels),
        inverse.reshape(-1, 1),
        norm_gain.reshape(1, channels),
        expand_bias.reshape(2, depth, 4, HIGH).transpose(2, 0, 1, 3).reshape(8, 1, WIDE),
        where,
    )
    weights_column, (scaled, masked, normed, inverse, gain, bias, where) = lax.optimization_barrier(
        (weights_column, ready)
    )
    first, second = sheets_of_weights(weights_column)
    scaled = lax.all_gather(scaled, "c", axis=0, tiled=True)
    masked = lax.all_gather(masked, "c", axis=0, tiled=True)
    back_mixed, gain_part, bias_part = pointwise(
        where, scaled, masked, normed, inverse, gain, bias, first, second
    )
    back_mixed = back_mixed.reshape(samples, row_count, col_count, channels)
    gain_part = gain_part.reshape(channels)
    bias_part = bias_part.reshape(-1)
    mixed_float = back_mixed.astype(jnp.float32)
    kernel_rows = []
    for shift_row in range(KS):
        band = padded[:, shift_row : shift_row + row_count, :, :]
        kernel_cols = [
            jnp.sum(
                band[:, :, shift_col : shift_col + col_count, :].astype(jnp.float32) * mixed_float,
                axis=(0, 1, 2),
            )
            for shift_col in range(KS)
        ]
        kernel_rows.append(jnp.stack(kernel_cols))
    kernel_part = jnp.stack(kernel_rows)
    back_padded = with_halo(back_mixed, rim)
    back_padded = jnp.pad(back_padded, ((0, 0), (0, 0), (rim, rim), (0, 0)))
    through = depthwise(back_padded, depth_kernel[::-1, ::-1], row_count, col_count)
    state_grad = (cotangent.astype(jnp.float32) + through).astype(jnp.bfloat16)
    kernel_grad, gain_grad, bias_grad = sum_everywhere((kernel_part, gain_part, bias_part))
    bias_grad = bias_grad.reshape(4, 2, depth, HIGH).transpose(1, 2, 0, 3).reshape(-1)
    return (state_grad, kernel_grad, gain_grad, bias_grad)


def solution(mesh):
    wide = Mesh(mesh.devices.reshape(2, 4, 2, 16, 2), ("yh", "x", "yl", "z", "c"))
    return jax.shard_map(
        local,
        mesh=wide,
        in_specs=(
            P(DP, TILE, None, None),
            P(DP, TILE, None, None),
            P(),
            P(),
            P(TILE, None),
            P(),
            P(TILE, None),
            P(TILE),
        ),
        out_specs=(P(DP, TILE, None, None), P(), P(), P()),
        check_vma=False,
    )
```

profile of v0, /device:TPU:1, one launch (start us, length us, event | category | flops | bytes accessed | tf_op | source)
XLA Modules:
  0.0 185.9 jit_solution(18312756163249118143)
XLA Ops:
  0.6 1.1 fusion.166
  1.8 4.9 %collective-permute-start = (bf16[1,3,64,768]{3,2,1,0:T(8,128)(2,1)S(1)}, bf16[1,3,64,768]{3,2,1,0:T(8,128)(2,1)S(1)}, u32[]{:S(2)}, u32[]{:S(2)}) collective-permute-start(bf16[1,3,64,768]{3,2,1,0:T(8,128)(2,1)S(1)} %get-tuple-element.151), channel_id=1, source_target_pairs={{0,1},{1,2},{2,3},{3,4},{4,5},{5,6},{6,7},{7,8},{8,9},{9,10},{10,1... | collective-permute-start | bytes 884744 | tf_op jit(solution)/shard_map/ppermute | solution.py:24
  6.7 5.1 %collective-permute-start.1 = (bf16[1,3,64,768]{3,2,1,0:T(8,128)(2,1)S(1)}, bf16[1,3,64,768]{3,2,1,0:T(8,128)(2,1)S(1)}, u32[]{:S(2)}, u32[]{:S(2)}) collective-permute-start(bf16[1,3,64,768]{3,2,1,0:T(8,128)(2,1)S(1)} %get-tuple-element.152), channel_id=1, source_target_pairs={{1,0},{2,1},{3,2},{4,3},{5,4},{6,5},{7,6},{8,7},{9,8},{10,9},{11,1... | collective-permute-start | bytes 884744 | tf_op jit(solution)/shard_map/ppermute | solution.py:26
  12.0 1.1 fusion.30
  13.1 2.0 %all-gather.1 = bf16[2,12,768]{2,1,0:T(8,128)(2,1)S(1)} all-gather(bf16[1,12,768]{2,1,0:T(8,128)(2,1)S(1)} %fusion.30), channel_id=2, replica_groups=mesh['yh'=2,'x'=4,'yl'=2,'z'=16,'c'=2] {'c'}, dimensions={0}, use_global_device_ids=true | all-gather | bytes 55296 | tf_op jit(solution)/shard_map/all_gather | solution.py:92
  16.6 12.8 %all-to-all-start = ((bf16[16,24,384]{2,1,0:T(8,128)(2,1)}), bf16[16,24,384]{2,1,0:T(8,128)(2,1)}, u32[]{:S(2)}, u32[]{:S(2)}) async-start(bf16[16,24,384]{2,1,0:T(8,128)(2,1)} %broadcast_in_dim.10), calls=%async_computation | async-start | bytes 589824 | tf_op jit(solution)/shard_map/all_to_all | solution.py:99
  31.0 6.5 %fusion.162 = (f32[4,64]{1,0:T(4,128)S(1)}, f32[1,4,64,768]{3,2,1,0:T(8,128)S(1)}) fusion(bf16[1,10,70,768]{3,2,1,0:T(8,128)(2,1)S(1)} %fusion.37, f32[768]{0:T(1024)S(1)} %get-tuple-element.92, f32[768]{0:T(1024)S(1)} %get-tuple-element.139, f32[768]{0:T(1024)S(1)} %get-tuple-element.140, ...), kind=kLoop, calls=%fused_computation.350 | loop fusion | flops 28901120 | bytes 20205568 | tf_op jit(solution)/shard_map/reduce_sum | solution.py:273
  38.0 5.8 %all-to-all-done = bf16[16,24,384]{2,1,0:T(8,128)(2,1)} async-done(((bf16[16,24,384]{2,1,0:T(8,128)(2,1)}), bf16[16,24,384]{2,1,0:T(8,128)(2,1)}, u32[]{:S(2)}, u32[]{:S(2)}) %all-to-all-start) | async-done | bytes 294944 | tf_op jit(solution)/shard_map/all_to_all | solution.py:99
  44.9 14.4 %all_to_all.25 = bf16[4,16,24,384]{3,2,1,0:T(8,128)(2,1)S(1)} all-to-all(bf16[4,16,24,384]{3,2,1,0:T(8,128)(2,1)S(1)} %broadcast_in_dim.11), channel_id=1, replica_groups=mesh['yh'=2,'x'=4,'yl'=2,'z'=16,'c'=2] {'yh','yl'}, dimensions={0} | all-to-all | bytes 2359296 | tf_op jit(solution)/shard_map/all_to_all | solution.py:104
  59.4 3.1 %collective-permute-start.3 = (bf16[768,384]{1,0:T(8,128)(2,1)S(1)}, bf16[768,384]{1,0:T(8,128)(2,1)S(1)}, u32[]{:S(2)}, u32[]{:S(2)}) collective-permute-start(bf16[768,384]{1,0:T(8,128)(2,1)S(1)} %bitcast.87), channel_id=1, source_target_pairs={{0,64},{64,0},{128,192},{192,128},{1,65},{65,1},{129,193},{193,129... | collective-permute-start | bytes 1769480 | tf_op jit(solution)/shard_map/ppermute | solution.py:108
  62.5 3.7 %collective-permute-start.5 = (bf16[768,384]{1,0:T(8,128)(2,1)S(1)}, bf16[768,384]{1,0:T(8,128)(2,1)S(1)}, u32[]{:S(2)}, u32[]{:S(2)}) collective-permute-start(bf16[768,384]{1,0:T(8,128)(2,1)S(1)} %bitcast.90), channel_id=1, source_target_pairs={{0,192},{192,0},{64,128},{128,64},{1,193},{193,1},{65,129},{129,65... | collective-permute-start | bytes 1769480 | tf_op jit(solution)/shard_map/ppermute | solution.py:109
  66.3 2.2 %collective-permute-start.7 = (bf16[768,384]{1,0:T(8,128)(2,1)S(1)}, bf16[768,384]{1,0:T(8,128)(2,1)S(1)}, u32[]{:S(2)}, u32[]{:S(2)}) collective-permute-start(bf16[768,384]{1,0:T(8,128)(2,1)S(1)} %bitcast.91), channel_id=1, source_target_pairs={{0,64},{64,0},{128,192},{192,128},{1,65},{65,1},{129,193},{193,129... | collective-permute-start | bytes 1769480 | tf_op jit(solution)/shard_map/ppermute | solution.py:110
  68.5 2.5 %collective-permute-start.2 = (bf16[768,384]{1,0:T(8,128)(2,1)S(1)}, bf16[768,384]{1,0:T(8,128)(2,1)S(1)}, u32[]{:S(2)}, u32[]{:S(2)}) collective-permute-start(bf16[768,384]{1,0:T(8,128)(2,1)S(1)} %bitcast.88), channel_id=1, source_target_pairs={{0,192},{192,0},{64,128},{128,64},{1,193},{193,1},{65,129},{129,65... | collective-permute-start | bytes 1769480 | tf_op jit(solution)/shard_map/ppermute | solution.py:111
  71.0 4.0 %collective-permute-start.4 = (bf16[768,384]{1,0:T(8,128)(2,1)S(1)}, bf16[768,384]{1,0:T(8,128)(2,1)S(1)}, u32[]{:S(2)}, u32[]{:S(2)}) collective-permute-start(bf16[768,384]{1,0:T(8,128)(2,1)S(1)} %collective-permute-done.3.s1), channel_id=1, source_target_pairs={{0,192},{192,0},{64,128},{128,64},{1,193},{193,1},{65,129},{129,65... | collective-permute-start | bytes 1769480 | tf_op jit(solution)/shard_map/ppermute | solution.py:112
  75.0 1.9 %collective-permute-start.6 = (bf16[768,384]{1,0:T(8,128)(2,1)S(1)}, bf16[768,384]{1,0:T(8,128)(2,1)S(1)}, u32[]{:S(2)}, u32[]{:S(2)}) collective-permute-start(bf16[768,384]{1,0:T(8,128)(2,1)S(1)} %collective-permute-done.5.s2), channel_id=1, source_target_pairs={{0,64},{64,0},{128,192},{192,128},{1,65},{65,1},{129,193},{193,129... | collective-permute-start | bytes 1769480 | tf_op jit(solution)/shard_map/ppermute | solution.py:113
  77.0 17.0 %all_gather.14.scaled_ref = bf16[512,768]{1,0:T(8,128)(2,1)S(1)} all-gather(bf16[256,768]{1,0:T(8,128)(2,1)S(1)} %bitcast.95), channel_id=1, replica_groups=mesh['yh'=2,'x'=4,'yl'=2,'z'=16,'c'=2] {'c'}, dimensions={0}, use_global_device_ids=true | all-gather | bytes 1179648 | tf_op jit(solution)/shard_map/all_gather | solution.py:294
  94.0 2.5 %all_gather.15.masked_ref = bf16[512,768]{1,0:T(8,128)(2,1)S(1)} all-gather(bf16[256,768]{1,0:T(8,128)(2,1)S(1)} %bitcast.94), channel_id=1, replica_groups=mesh['yh'=2,'x'=4,'yl'=2,'z'=16,'c'=2] {'c'}, dimensions={0}, use_global_device_ids=true | all-gather | bytes 1179648 | tf_op jit(solution)/shard_map/all_gather | solution.py:295
  96.5 5.1 %pointwise_first.1 = (f32[512,768]{1,0:T(8,128)S(1)}, f32[8,1,384]{2,1,0:T(1,128)S(1)}) custom-call(s32[2]{0:T(128)S(1)} %pad_add_fusion.where_ref, bf16[512,768]{1,0:T(8,128)(2,1)S(1)} %all_gather.14.scaled_ref, bf16[512,768]{1,0:T(8,128)(2,1)S(1)} %all_gather.15.masked_ref, f32[8,1,384]{2,1,0:T(1,128)S(1)} %reshape.428.bias_ref, ...), custom_call_target="tpu_custom_call" | custom-call | flops 1811939328 | bytes 20971520 | tf_op jit(solution)/shard_map/pointwise_first/pallas_call | solution.py:220
  101.7 6.2 %pointwise_second.1 = (f32[256,768]{1,0:T(8,128)S(1)}, f32[256,768]{1,0:T(8,128)}, f32[8,1,384]{2,1,0:T(1,128)S(1)}) custom-call(s32[2]{0:T(128)S(1)} %pad_add_fusion.where_ref, bf16[512,768]{1,0:T(8,128)(2,1)S(1)} %all_gather.14.scaled_ref, bf16[512,768]{1,0:T(8,128)(2,1)S(1)} %all_gather.15.masked_ref, f32[8,1,384]{2,1,0:T(1,128)S(1)} %reshape.428.bias_ref, ...), custom_call_target="tpu_custom_call" | custom-call | flops 1811939328 | bytes 20971520 | tf_op jit(solution)/shard_map/pointwise_second/pallas_call | solution.py:230
  107.8 6.9 %collective-permute-start.8 = (f32[256,768]{1,0:T(8,128)}, f32[256,768]{1,0:T(8,128)S(1)}, u32[]{:S(2)}, u32[]{:S(2)}) collective-permute-start(f32[256,768]{1,0:T(8,128)} %get-tuple-element.27), channel_id=1, source_target_pairs={{0,1},{1,0},{2,3},{3,2},{4,5},{5,4},{6,7},{7,6},{8,9},{9,8},{10,11... | collective-permute-start | bytes 2359304 | tf_op jit(solution)/shard_map/ppermute | solution.py:240
  115.6 1.3 collective-permute-done.8.other_ref
  117.9 1.9 %fusion.144 = (f32[768]{0:T(1024)S(1)}, f32[768]{0:T(1024)S(1)}, f32[768]{0:T(1024)S(1)}, f32[768]{0:T(1024)S(1)}, f32[768]{0:T(1024)S(1)}, /*index=5*/f32[768]{...) fusion(bf16[1,10,70,768]{3,2,1,0:T(8,128)(2,1)S(1)} %copy-done., ...), kind=kLoop, calls=%fused_computation.250 | loop fusion | flops 10799616 | bytes 7526400 | tf_op jit(solution)/shard_map/reduce_sum | solution.py:307
  119.9 1.1 fusion.141
  121.0 1.9 %fusion.123 = (f32[768]{0:T(1024)S(1)}, f32[768]{0:T(1024)S(1)}, f32[768]{0:T(1024)S(1)}, f32[768]{0:T(1024)S(1)}, f32[768]{0:T(1024)S(1)}, /*index=5*/f32[768]{...) fusion(bf16[1,10,70,768]{3,2,1,0:T(8,128)(2,1)S(1)} %copy-done., ...), kind=kLoop, calls=%fused_computation.229 | loop fusion | flops 10799616 | bytes 7526400 | tf_op jit(solution)/shard_map/reduce_sum | solution.py:307
  124.2 13.1 %all_to_all.26 = f32[32,16,128]{2,1,0:T(8,128)S(1)} all-to-all(f32[32,16,128]{2,1,0:T(8,128)S(1)} %bitcast.96), channel_id=1, replica_groups=mesh['yh'=2,'x'=4,'yl'=2,'z'=16,'c'=2] {'yh','x','yl','c'}, dimensions={0} | all-to-all | bytes 524288 | tf_op jit(solution)/shard_map/all_to_all | solution.py:63
  138.0 16.4 %all-to-all-start.3 = ((f32[16,16,128]{2,1,0:T(8,128)}), f32[16,16,128]{2,1,0:T(8,128)S(1)}, u32[]{:S(2)}, u32[]{:S(2)}) async-start(f32[16,16,128]{2,1,0:T(8,128)} %broadcast_in_dim.13), calls=%async_computation.3 | async-start | bytes 262144 | tf_op jit(solution)/shard_map/all_to_all | solution.py:65
  154.6 3.3 %collective-permute-start.10 = (bf16[1,3,64,768]{3,2,1,0:T(8,128)(2,1)S(1)}, bf16[1,3,64,768]{3,2,1,0:T(8,128)(2,1)S(1)}, u32[]{:S(2)}, u32[]{:S(2)}) collective-permute-start(bf16[1,3,64,768]{3,2,1,0:T(8,128)(2,1)S(1)} %get-tuple-element.148), channel_id=1, source_target_pairs={{1,0},{2,1},{3,2},{4,3},{5,4},{6,5},{7,6},{8,7},{9,8},{10,9},{11,1... | collective-permute-start | bytes 884744 | tf_op jit(solution)/shard_map/ppermute | solution.py:26
  157.9 3.4 %collective-permute-start.9 = (bf16[1,3,64,768]{3,2,1,0:T(8,128)(2,1)S(1)}, bf16[1,3,64,768]{3,2,1,0:T(8,128)(2,1)S(1)}, u32[]{:S(2)}, u32[]{:S(2)}) collective-permute-start(bf16[1,3,64,768]{3,2,1,0:T(8,128)(2,1)S(1)} %get-tuple-element.147), channel_id=1, source_target_pairs={{0,1},{1,2},{2,3},{3,4},{4,5},{5,6},{6,7},{7,8},{8,9},{9,10},{10,1... | collective-permute-start | bytes 884744 | tf_op jit(solution)/shard_map/ppermute | solution.py:24
  161.3 5.2 %collective-permute-done.10 = bf16[1,3,64,768]{3,2,1,0:T(8,128)(2,1)S(1)} collective-permute-done((bf16[1,3,64,768]{3,2,1,0:T(8,128)(2,1)S(1)}, bf16[1,3,64,768]{3,2,1,0:T(8,128)(2,1)S(1)}, u32[]{:S(2)}, u32[]{:S(2)}) %collective-permute-start.10) | collective-permute-done | bytes 294944 | tf_op jit(solution)/shard_map/ppermute | solution.py:26
  167.6 7.3 %all-to-all-start.4 = ((f32[32,16,128]{2,1,0:T(8,128)}), f32[32,16,128]{2,1,0:T(8,128)S(1)}, u32[]{:S(2)}, u32[]{:S(2)}) async-start(f32[32,16,128]{2,1,0:T(8,128)} %broadcast_in_dim.14), calls=%async_computation.4 | async-start | bytes 524288 | tf_op jit(solution)/shard_map/all_to_all | solution.py:67
  175.0 6.5 %fusion.95 = bf16[1,4,64,768]{3,2,1,0:T(8,128)(2,1)} fusion(bf16[1,4,64,768]{3,2,1,0:T(8,128)(2,1)S(1)} %bitcast.85, bf16[1,4,64,768]{3,2,1,0:T(8,128)(2,1)S(1)} %copy-done.9, bf16[1,3,64,768]{3,2,1,0:T(8,128)(2,1)S(1)} %collective-permute-done.10, bf16[1,3,64,768]{3,2,1,0:T(8,128)(2,1)S(1)} %collective-permute-done.9, ...), kind=kLoop, calls=%fused_computation.201 | loop fusion | flops 30474240 | bytes 18435072 | tf_op jit(solution)/shard_map/convert_element_type | solution.py:318
  181.5 2.2 %all-to-all-done.4 = f32[32,16,128]{2,1,0:T(8,128)S(1)} async-done(((f32[32,16,128]{2,1,0:T(8,128)}), f32[32,16,128]{2,1,0:T(8,128)S(1)}, u32[]{:S(2)}, u32[]{:S(2)}) %all-to-all-start.4) | async-done | bytes 262176 | tf_op jit(solution)/shard_map/all_to_all | solution.py:67
  (191 shorter events, 11.1 us)
Async XLA Ops:
  0.6 11.3 %copy-start = (bf16[12,3072]{1,0:T(8,128)(2,1)S(1)}, bf16[12,3072]{1,0:T(8,128)(2,1)}, u32[]{:S(2)}) copy-start(bf16[12,3072]{1,0:T(8,128)(2,1)} %param.12) | copy-start | bytes 221188
  1.8 28.7 %collective-permute-start = (bf16[1,3,64,768]{3,2,1,0:T(8,128)(2,1)S(1)}, bf16[1,3,64,768]{3,2,1,0:T(8,128)(2,1)S(1)}, u32[]{:S(2)}, u32[]{:S(2)}) collective-permute-start(bf16[1,3,64,768]{3,2,1,0:T(8,128)(2,1)S(1)} %get-tuple-element.151), channel_id=1, source_target_pairs={{0,1},{1,2},{2,3},{3,4},{4,5},{5,6},{6,7},{7,8},{8,9},{9,10},{10,1... | collective-permute-start | bytes 884744 | tf_op jit(solution)/shard_map/ppermute | solution.py:24
  6.7 23.8 %collective-permute-start.1 = (bf16[1,3,64,768]{3,2,1,0:T(8,128)(2,1)S(1)}, bf16[1,3,64,768]{3,2,1,0:T(8,128)(2,1)S(1)}, u32[]{:S(2)}, u32[]{:S(2)}) collective-permute-start(bf16[1,3,64,768]{3,2,1,0:T(8,128)(2,1)S(1)} %get-tuple-element.152), channel_id=1, source_target_pairs={{1,0},{2,1},{3,2},{4,3},{5,4},{6,5},{7,6},{8,7},{9,8},{10,9},{11,1... | collective-permute-start | bytes 884744 | tf_op jit(solution)/shard_map/ppermute | solution.py:26
  11.9 17.4 %copy-start.10 = (f32[7,7,768]{2,1,0:T(8,128)S(1)}, f32[7,7,768]{2,1,0:T(8,128)}, u32[]{:S(2)}) copy-start(f32[7,7,768]{2,1,0:T(8,128)} %param.10) | copy-start | bytes 451588
  12.0 17.6 %copy-start.34 = (s32[4]{0:T(128)S(1)}, s32[4]{0:T(128)}, u32[]{:S(2)}) copy-start(s32[4]{0:T(128)} %param.15) | copy-start | bytes 52
  12.0 17.6 %copy-start.8 = (bf16[1,4,64,768]{3,2,1,0:T(8,128)(2,1)S(1)}, bf16[1,4,64,768]{3,2,1,0:T(8,128)(2,1)}, u32[]{:S(2)}) copy-start(bf16[1,4,64,768]{3,2,1,0:T(8,128)(2,1)} %param.9) | copy-start | bytes 1179652
  13.1 17.1 %copy-start.32 = (f32[3072]{0:T(1024)S(1)}, f32[3072]{0:T(1024)}, u32[]{:S(2)}) copy-start(f32[3072]{0:T(1024)} %param.13) | copy-start | bytes 36868
  13.1 17.4 %copy-start.31 = (f32[768]{0:T(1024)S(1)}, f32[768]{0:T(1024)}, u32[]{:S(2)}) copy-start(f32[768]{0:T(1024)} %param.11) | copy-start | bytes 9220
  13.1 17.4 %copy-start.3 = (bf16[1,4,64,768]{3,2,1,0:T(8,128)(2,1)S(1)}, bf16[1,4,64,768]{3,2,1,0:T(8,128)(2,1)}, u32[]{:S(2)}) copy-start(bf16[1,4,64,768]{3,2,1,0:T(8,128)(2,1)} %param.8) | copy-start | bytes 1179652
  16.6 27.2 %all-to-all-start = ((bf16[16,24,384]{2,1,0:T(8,128)(2,1)}), bf16[16,24,384]{2,1,0:T(8,128)(2,1)}, u32[]{:S(2)}, u32[]{:S(2)}) async-start(bf16[16,24,384]{2,1,0:T(8,128)(2,1)} %broadcast_in_dim.10), calls=%async_computation | async-start | bytes 589824 | tf_op jit(solution)/shard_map/all_to_all | solution.py:99
  59.4 11.6 %collective-permute-start.3 = (bf16[768,384]{1,0:T(8,128)(2,1)S(1)}, bf16[768,384]{1,0:T(8,128)(2,1)S(1)}, u32[]{:S(2)}, u32[]{:S(2)}) collective-permute-start(bf16[768,384]{1,0:T(8,128)(2,1)S(1)} %bitcast.87), channel_id=1, source_target_pairs={{0,64},{64,0},{128,192},{192,128},{1,65},{65,1},{129,193},{193,129... | collective-permute-start | bytes 1769480 | tf_op jit(solution)/shard_map/ppermute | solution.py:108
  62.5 12.5 %collective-permute-start.5 = (bf16[768,384]{1,0:T(8,128)(2,1)S(1)}, bf16[768,384]{1,0:T(8,128)(2,1)S(1)}, u32[]{:S(2)}, u32[]{:S(2)}) collective-permute-start(bf16[768,384]{1,0:T(8,128)(2,1)S(1)} %bitcast.90), channel_id=1, source_target_pairs={{0,192},{192,0},{64,128},{128,64},{1,193},{193,1},{65,129},{129,65... | collective-permute-start | bytes 1769480 | tf_op jit(solution)/shard_map/ppermute | solution.py:109
  66.3 30.2 %collective-permute-start.7 = (bf16[768,384]{1,0:T(8,128)(2,1)S(1)}, bf16[768,384]{1,0:T(8,128)(2,1)S(1)}, u32[]{:S(2)}, u32[]{:S(2)}) collective-permute-start(bf16[768,384]{1,0:T(8,128)(2,1)S(1)} %bitcast.91), channel_id=1, source_target_pairs={{0,64},{64,0},{128,192},{192,128},{1,65},{65,1},{129,193},{193,129... | collective-permute-start | bytes 1769480 | tf_op jit(solution)/shard_map/ppermute | solution.py:110
  68.5 33.1 %collective-permute-start.2 = (bf16[768,384]{1,0:T(8,128)(2,1)S(1)}, bf16[768,384]{1,0:T(8,128)(2,1)S(1)}, u32[]{:S(2)}, u32[]{:S(2)}) collective-permute-start(bf16[768,384]{1,0:T(8,128)(2,1)S(1)} %bitcast.88), channel_id=1, source_target_pairs={{0,192},{192,0},{64,128},{128,64},{1,193},{193,1},{65,129},{129,65... | collective-permute-start | bytes 1769480 | tf_op jit(solution)/shard_map/ppermute | solution.py:111
  71.0 30.6 %collective-permute-start.4 = (bf16[768,384]{1,0:T(8,128)(2,1)S(1)}, bf16[768,384]{1,0:T(8,128)(2,1)S(1)}, u32[]{:S(2)}, u32[]{:S(2)}) collective-permute-start(bf16[768,384]{1,0:T(8,128)(2,1)S(1)} %collective-permute-done.3.s1), channel_id=1, source_target_pairs={{0,192},{192,0},{64,128},{128,64},{1,193},{193,1},{65,129},{129,65... | collective-permute-start | bytes 1769480 | tf_op jit(solution)/shard_map/ppermute | solution.py:112
  75.0 26.6 %collective-permute-start.6 = (bf16[768,384]{1,0:T(8,128)(2,1)S(1)}, bf16[768,384]{1,0:T(8,128)(2,1)S(1)}, u32[]{:S(2)}, u32[]{:S(2)}) collective-permute-start(bf16[768,384]{1,0:T(8,128)(2,1)S(1)} %collective-permute-done.5.s2), channel_id=1, source_target_pairs={{0,64},{64,0},{128,192},{192,128},{1,65},{65,1},{129,193},{193,129... | collective-permute-start | bytes 1769480 | tf_op jit(solution)/shard_map/ppermute | solution.py:113
  107.8 9.0 %collective-permute-start.8 = (f32[256,768]{1,0:T(8,128)}, f32[256,768]{1,0:T(8,128)S(1)}, u32[]{:S(2)}, u32[]{:S(2)}) collective-permute-start(f32[256,768]{1,0:T(8,128)} %get-tuple-element.27), channel_id=1, source_target_pairs={{0,1},{1,0},{2,3},{3,2},{4,5},{5,4},{6,7},{7,6},{8,9},{9,8},{10,11... | collective-permute-start | bytes 2359304 | tf_op jit(solution)/shard_map/ppermute | solution.py:240
  138.0 28.8 %all-to-all-start.3 = ((f32[16,16,128]{2,1,0:T(8,128)}), f32[16,16,128]{2,1,0:T(8,128)S(1)}, u32[]{:S(2)}, u32[]{:S(2)}) async-start(f32[16,16,128]{2,1,0:T(8,128)} %broadcast_in_dim.13), calls=%async_computation.3 | async-start | bytes 262144 | tf_op jit(solution)/shard_map/all_to_all | solution.py:65
  154.5 20.4 %copy-start.9 = (bf16[1,4,64,768]{3,2,1,0:T(8,128)(2,1)S(1)}, bf16[1,4,64,768]{3,2,1,0:T(8,128)(2,1)}, u32[]{:S(2)}) copy-start(bf16[1,4,64,768]{3,2,1,0:T(8,128)(2,1)} %param.9) | copy-start | bytes 1179652
  154.5 20.4 %copy-start.12 = (f32[768]{0:T(1024)S(1)}, f32[768]{0:T(1024)}, u32[]{:S(2)}) copy-start(f32[768]{0:T(1024)} %copy-done.11) | copy-start | bytes 9220
  154.5 20.4 %copy-start.14 = (f32[768]{0:T(1024)S(1)}, f32[768]{0:T(1024)}, u32[]{:S(2)}) copy-start(f32[768]{0:T(1024)} %copy-done.13) | copy-start | bytes 9220
  154.5 20.4 %copy-start.16 = (f32[768]{0:T(1024)S(1)}, f32[768]{0:T(1024)}, u32[]{:S(2)}) copy-start(f32[768]{0:T(1024)} %copy-done.15) | copy-start | bytes 9220
  154.6 20.4 %copy-start.18 = (f32[768]{0:T(1024)S(1)}, f32[768]{0:T(1024)}, u32[]{:S(2)}) copy-start(f32[768]{0:T(1024)} %copy-done.17) | copy-start | bytes 9220
  154.6 20.4 %copy-start.20 = (f32[768]{0:T(1024)S(1)}, f32[768]{0:T(1024)}, u32[]{:S(2)}) copy-start(f32[768]{0:T(1024)} %copy-done.19) | copy-start | bytes 9220
  154.6 20.4 %copy-start.22 = (f32[768]{0:T(1024)S(1)}, f32[768]{0:T(1024)}, u32[]{:S(2)}) copy-start(f32[768]{0:T(1024)} %copy-done.21) | copy-start | bytes 9220
  154.6 20.4 %copy-start.24 = (f32[768]{0:T(1024)S(1)}, f32[768]{0:T(1024)}, u32[]{:S(2)}) copy-start(f32[768]{0:T(1024)} %copy-done.23) | copy-start | bytes 9220
  154.6 20.4 %copy-start.26 = (f32[768]{0:T(1024)S(1)}, f32[768]{0:T(1024)}, u32[]{:S(2)}) copy-start(f32[768]{0:T(1024)} %copy-done.25) | copy-start | bytes 9220
  154.6 20.4 %copy-start.28 = (f32[768]{0:T(1024)S(1)}, f32[768]{0:T(1024)}, u32[]{:S(2)}) copy-start(f32[768]{0:T(1024)} %copy-done.27) | copy-start | bytes 9220
  154.6 20.4 %copy-start.30 = (f32[768]{0:T(1024)S(1)}, f32[768]{0:T(1024)}, u32[]{:S(2)}) copy-start(f32[768]{0:T(1024)} %copy-done.29) | copy-start | bytes 9220
  154.6 11.9 %collective-permute-start.10 = (bf16[1,3,64,768]{3,2,1,0:T(8,128)(2,1)S(1)}, bf16[1,3,64,768]{3,2,1,0:T(8,128)(2,1)S(1)}, u32[]{:S(2)}, u32[]{:S(2)}) collective-permute-start(bf16[1,3,64,768]{3,2,1,0:T(8,128)(2,1)S(1)} %get-tuple-element.148), channel_id=1, source_target_pairs={{1,0},{2,1},{3,2},{4,3},{5,4},{6,5},{7,6},{8,7},{9,8},{10,9},{11,1... | collective-permute-start | bytes 884744 | tf_op jit(solution)/shard_map/ppermute | solution.py:26
  157.9 8.6 %collective-permute-start.9 = (bf16[1,3,64,768]{3,2,1,0:T(8,128)(2,1)S(1)}, bf16[1,3,64,768]{3,2,1,0:T(8,128)(2,1)S(1)}, u32[]{:S(2)}, u32[]{:S(2)}) collective-permute-start(bf16[1,3,64,768]{3,2,1,0:T(8,128)(2,1)S(1)} %get-tuple-element.147), channel_id=1, source_target_pairs={{0,1},{1,2},{2,3},{3,4},{4,5},{5,6},{6,7},{7,8},{8,9},{9,10},{10,1... | collective-permute-start | bytes 884744 | tf_op jit(solution)/shard_map/ppermute | solution.py:24
  167.6 16.1 %all-to-all-start.4 = ((f32[32,16,128]{2,1,0:T(8,128)}), f32[32,16,128]{2,1,0:T(8,128)S(1)}, u32[]{:S(2)}, u32[]{:S(2)}) async-start(f32[32,16,128]{2,1,0:T(8,128)} %broadcast_in_dim.14), calls=%async_computation.4 | async-start | bytes 524288 | tf_op jit(solution)/shard_map/all_to_all | solution.py:67
  (17 other events, 38.9 us)
where the time goes:
time: 187 us; the launch traced here: 186 us
  starting transfers between devices  77.7 us (42%)
  blocking collectives  49.1 us (26%)
  other arithmetic  20.2 us (11%)
  waiting for transfers between devices  14.4 us (8%)
  Pallas kernels  12.3 us (7%)
  local copies, waits for them, and re-layouts  9 us (5%)
  between operations  2.13 us (1%)
    all_gather x1, blocking collectives, local(): scaled = lax.all_gather(scaled, 'c', axis=0, tiled=True)  17 us
    all_to_all x1, starting transfers between devices, sum_everywhere(): mine = jnp.sum(lax.all_to_all(mine, 'z', 0, 0), axis=0)  16.4 us
    all_to_all x1, blocking collectives, sheets_of_weights(): lax.all_to_all(jnp.broadcast_to(column[None], (4, depth, HIGH, WIDE)), ('...  14.4 us
    all_to_all x1, blocking collectives, sum_everywhere(): mine = jnp.sum(lax.all_to_all(stacked, PLANE, 0, 0), axis=0)  13.1 us
    all_to_all x1, starting transfers between devices, column_of_weights(): lax.all_to_all(jnp.broadcast_to(piece[None], (depth, HIGH, WIDE)), 'z', 0...  12.8 us
    ppermute x2, starting transfers between devices, with_halo(): lax.ppermute(head, TILE, [(i + 1, i) for i in range(ends)])  8.39 us
    ppermute x2, starting transfers between devices, with_halo(): lax.ppermute(tail, TILE, [(i, i + 1) for i in range(ends)])  8.37 us
    all_to_all x1, starting transfers between devices, sum_everywhere(): full = lax.all_to_all(mine, PLANE, 0, 0).reshape(plane * share, lanes)  7.29 us
  transfers between devices with their start and end apart: 14, of which 4 were waited for; matrix products, arithmetic and copies ran while one was open for 10% of the time, Pallas kernels for 3%

commit v1 on v0

--- a/solution.py
+++ b/solution.py
@@ -9,24 +9,26 @@
 from jax.sharding import PartitionSpec as P
 
 KS = 7
+LANES = 128
 TILE = ("yl", "z", "c")
 DP = ("yh", "x")
 PLANE = ("yh", "x", "yl", "c")
 
 
-def with_halo(cells, width):
+def exchange_rims(cells, width):
     count = lax.axis_size(TILE)
     ends = count - 1
     head = lax.slice_in_dim(cells, 0, width, axis=1)
     tail = lax.slice_in_dim(cells, cells.shape[1] - width, cells.shape[1], axis=1)
-    return jnp.concatenate(
-        [
-            lax.ppermute(tail, TILE, [(i, i + 1) for i in range(ends)]),
-            cells,
-            lax.ppermute(head, TILE, [(i + 1, i) for i in range(ends)]),
-        ],
-        axis=1,
-    )
+    return (
+        lax.ppermute(tail, TILE, [(i, i + 1) for i in range(ends)]),
+        lax.ppermute(head, TILE, [(i + 1, i) for i in range(ends)]),
+    )
+
+
+def join_rims(cells, rims, width):
+    padded = jnp.concatenate([rims[0], cells, rims[1]], axis=1)
+    return jnp.pad(padded, ((0, 0), (0, 0), (width, width), (0, 0)))
 
 
 def depthwise(padded, kernel, row_count, col_count):
@@ -51,23 +53,27 @@
     )
 
 
-def sum_everywhere(parts):
-    lanes = 128
+def sum_shares(parts):
     plane = lax.axis_size(PLANE)
     depth = lax.axis_size("z")
-    rows = [part.reshape(-1, lanes) for part in parts]
+    rows = [part.reshape(-1, LANES) for part in parts]
     used = sum(piece.shape[0] for piece in rows)
     share = -(-used // (8 * plane)) * 8
-    rows.append(jnp.zeros((share * plane - used, lanes), jnp.float32))
-    stacked = jnp.concatenate(rows).reshape(plane, share, lanes)
+    rows.append(jnp.zeros((share * plane - used, LANES), jnp.float32))
+    stacked = jnp.concatenate(rows).reshape(plane, share, LANES)
     mine = jnp.sum(lax.all_to_all(stacked, PLANE, 0, 0), axis=0)
-    mine = jnp.broadcast_to(mine[None], (depth, share, lanes))
-    mine = jnp.sum(lax.all_to_all(mine, "z", 0, 0), axis=0)
-    mine = jnp.broadcast_to(mine[None], (plane, share, lanes))
-    full = lax.all_to_all(mine, PLANE, 0, 0).reshape(plane * share, lanes)
+    mine = jnp.broadcast_to(mine[None], (depth, share, LANES))
+    return lax.all_to_all(mine, "z", 0, 0)
+
+
+def gather_sums(shares, parts):
+    plane = lax.axis_size(PLANE)
+    mine = jnp.sum(shares, axis=0)
+    full = lax.all_to_all(jnp.broadcast_to(mine[None], (plane, *mine.shape)), PLANE, 0, 0)
+    full = full.reshape(-1, LANES)
     out, start = [], 0
     for part in parts:
-        count = part.size // lanes
+        count = part.size // LANES
         out.append(full[start : start + count].reshape(part.shape))
         start += count
     return out
@@ -99,11 +105,11 @@
     return lax.all_to_all(jnp.broadcast_to(piece[None], (depth, HIGH, WIDE)), "z", 0, 0)
 
 
-def sheets_of_weights(column):
+def sheets_of_weights(column, scaled, masked):
     depth = column.shape[0]
-    own = lax.all_to_all(
-        jnp.broadcast_to(column[None], (4, depth, HIGH, WIDE)), ("yh", "yl"), 0, 0
-    ).reshape(2, 2 * depth * HIGH, WIDE)
+    own = lax.all_to_all(jnp.broadcast_to(column[None], (4, depth, HIGH, WIDE)), ("yh", "yl"), 0, 0)
+    own = own.reshape(2, 2 * depth * HIGH, WIDE)
+    own, scaled, masked = lax.optimization_barrier((own, scaled, masked))
     own_expand, own_reduce = own[0], own[1]
     near_expand = lax.ppermute(own_expand, "x", NEAR)
     far_reduce = lax.ppermute(own_reduce, "x", FAR)
@@ -111,38 +117,25 @@
     far_expand = lax.ppermute(own_expand, "x", FAR)
     across_expand = lax.ppermute(near_expand, "x", FAR)
     across_reduce = lax.ppermute(far_reduce, "x", NEAR)
-    return (own_expand, near_expand, own_reduce, near_reduce), (
-        far_expand,
-        across_expand,
-        far_reduce,
-        across_reduce,
-    )
-
-
-def add_band(band, first_side, scaled_ref, masked_ref, bias_ref, sheets, bias_out, expand, reduce, sem, total):
-    wide = expand.shape[2]
+    scaled = lax.all_gather(scaled, "c", axis=0, tiled=True)
+    masked = lax.all_gather(masked, "c", axis=0, tiled=True)
+    first = own_expand, near_expand, own_reduce, near_reduce
+    second = far_expand, across_expand, far_reduce, across_reduce
+    return first, second, scaled, masked
+
+
+def add_band(band, first_side, scaled_ref, masked_ref, bias_ref, expand, reduce, bias_out, total):
     contract_last = (((1,), (1,)), ((), ()))
-    copies = [
-        pltpu.make_async_copy(sheets[0], expand.at[0], sem.at[0]),
-        pltpu.make_async_copy(sheets[2], reduce.at[0], sem.at[2]),
-        pltpu.make_async_copy(sheets[3], reduce.at[1], sem.at[3]),
-        pltpu.make_async_copy(sheets[1], expand.at[1], sem.at[1]),
-    ]
-    for copy in copies:
-        copy.start()
     sides = (first_side, 1 - first_side)
     for part in range(2):
-        half = pl.ds(pl.multiple_of(sides[part] * wide, wide), wide)
-        copies[3 if part else 0].wait()
-        hidden = jnp.dot(scaled_ref[...], expand[part], preferred_element_type=jnp.float32)
+        half = pl.ds(pl.multiple_of(sides[part] * WIDE, WIDE), WIDE)
+        hidden = jnp.dot(scaled_ref[...], expand[part][...], preferred_element_type=jnp.float32)
         slope = gelu_slope(hidden + bias_ref[band * 2 + sides[part]])
         back_act = None
         for other in range(2):
-            if part == 0:
-                copies[1 + other].wait()
             term = lax.dot_general(
-                masked_ref[:, pl.ds(pl.multiple_of(sides[other] * wide, wide), wide)],
-                reduce[other, half, :],
+                masked_ref[:, pl.ds(pl.multiple_of(sides[other] * WIDE, WIDE), WIDE)],
+                reduce[other][half, :],
                 contract_last,
                 preferred_element_type=jnp.float32,
             )
@@ -150,25 +143,23 @@
         back_hidden = (back_act * slope).astype(jnp.bfloat16)
         bias_out[band * 2 + sides[part]] = jnp.sum(back_hidden.astype(jnp.float32), axis=0, keepdims=True)
         total[...] += lax.dot_general(
-            back_hidden, expand[part], contract_last, preferred_element_type=jnp.float32
+            back_hidden, expand[part][...], contract_last, preferred_element_type=jnp.float32
         )
 
 
-def first_body(
-    where_ref, scaled_ref, masked_ref, bias_ref, s0, s1, s2, s3, total_ref, bias_out, expand, reduce, sem
-):
+def first_body(where_ref, scaled_ref, masked_ref, bias_ref, e0, e1, r0, r1, total_ref, bias_out):
     column, core = where_ref[0], where_ref[1]
     bias_out[...] = jnp.zeros_like(bias_out)
     total_ref[...] = jnp.zeros_like(total_ref)
     add_band(
         2 * core + lax.div(column, 2), lax.rem(column, 2), scaled_ref, masked_ref, bias_ref,
-        (s0, s1, s2, s3), bias_out, expand, reduce, sem, total_ref,
+        (e0, e1), (r0, r1), bias_out, total_ref,
     )
 
 
 def second_body(
-    where_ref, scaled_ref, masked_ref, bias_ref, s0, s1, s2, s3, sum_ref, bias_in,
-    mine_ref, other_ref, bias_out, expand, reduce, total, sem,
+    where_ref, scaled_ref, masked_ref, bias_ref, e0, e1, r0, r1, sum_ref, bias_in,
+    mine_ref, other_ref, bias_out, total,
 ):
     column, core = where_ref[0], where_ref[1]
     cells = mine_ref.shape[0]
@@ -176,7 +167,7 @@
     total[...] = sum_ref[...]
     add_band(
         2 * core + 1 - lax.div(column, 2), 1 - lax.rem(column, 2), scaled_ref, masked_ref, bias_ref,
-        (s0, s1, s2, s3), bias_out, expand, reduce, sem, total,
+        (e0, e1), (r0, r1), bias_out, total,
     )
     mine_ref[...] = total[pl.ds(pl.multiple_of(core * cells, cells), cells), :]
     other_ref[...] = total[pl.ds(pl.multiple_of((1 - core) * cells, cells), cells), :]
@@ -206,10 +197,7 @@
 def pointwise(where, scaled, masked, normed, inverse, gain, bias, first, second):
     cells, channels = normed.shape
     vmem = pl.BlockSpec(memory_space=pltpu.VMEM)
-    there = pl.BlockSpec(memory_space=pl.ANY)
     smem = pl.BlockSpec(memory_space=pltpu.SMEM)
-    weights = [pltpu.VMEM((2, channels, WIDE), jnp.bfloat16) for _ in range(2)]
-    sem = pltpu.SemaphoreType.DMA((4,))
     whole = jax.ShapeDtypeStruct((2 * cells, channels), jnp.float32)
     half = jax.ShapeDtypeStruct((cells, channels), jnp.float32)
     bias_shape = jax.ShapeDtypeStruct(bias.shape, jnp.float32)
@@ -220,9 +208,8 @@
     total, bias_part = pl.pallas_call(
         first_body,
         out_shape=(whole, bias_shape),
-        in_specs=[smem] + [vmem] * 3 + [there] * 4,
+        in_specs=[smem] + [vmem] * 7,
         out_specs=(vmem, vmem),
-        scratch_shapes=weights + [sem],
         compiler_params=params,
         cost_estimate=cost,
         name="pointwise_first",
@@ -230,9 +217,9 @@
     mine, other, bias_part = pl.pallas_call(
         second_body,
         out_shape=(half, half, bias_shape),
-        in_specs=[smem] + [vmem] * 3 + [there] * 4 + [vmem] * 2,
+        in_specs=[smem] + [vmem] * 9,
         out_specs=(vmem, vmem, vmem),
-        scratch_shapes=weights + [pltpu.VMEM((2 * cells, channels), jnp.float32), sem],
+        scratch_shapes=[pltpu.VMEM((2 * cells, channels), jnp.float32)],
         compiler_params=params,
         cost_estimate=cost,
         name="pointwise_second",
@@ -267,8 +254,8 @@
     tile_rows = row_count // tile_count
     rim = KS // 2
     weights_column = column_of_weights(expand_weight, reduce_weight)
-    padded = with_halo(ocean_state, rim)
-    padded = jnp.pad(padded, ((0, 0), (0, 0), (rim, rim), (0, 0)))
+    rims = exchange_rims(ocean_state, rim)
+    padded = join_rims(ocean_state, rims, rim)
     mixed = depthwise(padded, depth_kernel, row_count, col_count)
     centred = mixed - jnp.mean(mixed, axis=-1, keepdims=True)
     inverse = lax.rsqrt(jnp.mean(centred * centred, axis=-1, keepdims=True) + 1e-06)
@@ -287,12 +274,8 @@
         expand_bias.reshape(2, depth, 4, HIGH).transpose(2, 0, 1, 3).reshape(8, 1, WIDE),
         where,
     )
-    weights_column, (scaled, masked, normed, inverse, gain, bias, where) = lax.optimization_barrier(
-        (weights_column, ready)
-    )
-    first, second = sheets_of_weights(weights_column)
-    scaled = lax.all_gather(scaled, "c", axis=0, tiled=True)
-    masked = lax.all_gather(masked, "c", axis=0, tiled=True)
+    scaled, masked, normed, inverse, gain, bias, where = ready
+    first, second, scaled, masked = sheets_of_weights(weights_column, scaled, masked)
     back_mixed, gain_part, bias_part = pointwise(
         where, scaled, masked, normed, inverse, gain, bias, first, second
     )
@@ -312,11 +295,13 @@
         ]
         kernel_rows.append(jnp.stack(kernel_cols))
     kernel_part = jnp.stack(kernel_rows)
-    back_padded = with_halo(back_mixed, rim)
-    back_padded = jnp.pad(back_padded, ((0, 0), (0, 0), (rim, rim), (0, 0)))
+    rims = exchange_rims(back_mixed, rim)
+    parts = kernel_part, gain_part, bias_part
+    shares = sum_shares(parts)
+    back_padded = join_rims(back_mixed, rims, rim)
     through = depthwise(back_padded, depth_kernel[::-1, ::-1], row_count, col_count)
     state_grad = (cotangent.astype(jnp.float32) + through).astype(jnp.bfloat16)
-    kernel_grad, gain_grad, bias_grad = sum_everywhere((kernel_part, gain_part, bias_part))
+    kernel_grad, gain_grad, bias_grad = gather_sums(shares, parts)
     bias_grad = bias_grad.reshape(4, 2, depth, HIGH).transpose(1, 2, 0, 3).reshape(-1)
     return (state_grad, kernel_grad, gain_grad, bias_grad)
 

time: 187 us -> 190 us (1.016)
  blocking collectives: 49.1 us -> 35.2 us
  waiting for transfers between devices: 14.4 us -> 21.3 us
  local copies, waits for them, and re-layouts: 9 us -> 13.4 us
  starting transfers between devices: 77.7 us -> 81.9 us
  other arithmetic: 20.2 us -> 22.8 us
    all_to_all x2 -> x1, blocking collectives: 27.6 us -> 13.2 us  [sum_shares(): mine = jnp.sum(lax.all_to_all(stacked, PLANE, 0, 0), axis=0)]
    all_to_all x2 -> x3, starting transfers between devices: 23.7 us -> 28.1 us  [the longest x1 16.5 us: sum_shares(): return lax.all_to_all(mine, 'z', 0, 0)]
    all_to_all x1, waiting for transfers between devices: 5.76 us -> 9.61 us  [column_of_weights(): lax.all_to_all(jnp.broadcast_to(piece[None], (depth, HIGH, WIDE)), 'z', 0...]
    unnamed x77 -> x145, local copies, waits for them, and re-layouts: 0.22 us -> 2.97 us
    all_to_all x2 -> x3, waiting for transfers between devices: 2.18 us -> 4.62 us  [the longest x1 2.57 us: sheets_of_weights(): lax.all_to_all(jnp.broadcast_to(column[None], (4, depth, HIGH, WIDE)), ('...]
  transfers between devices with their start and end apart: 14 -> 15, of which waited for: 4 -> 5; matrix products, arithmetic and copies ran while one was open for 10% -> 11% of each run, Pallas kernels for 3% -> 2%
where the time goes in v1:
time: 190 us; the launch traced here: 189 us
  starting transfers between devices  81.9 us (43%)
  blocking collectives  35.2 us (19%)
  other arithmetic  22.8 us (12%)
  waiting for transfers between devices  21.3 us (11%)
  local copies, waits for them, and re-layouts  13.4 us (7%)
  Pallas kernels  11.2 us (6%)
  between operations  2.58 us (1%)
    all_gather x1, blocking collectives, sheets_of_weights(): scaled = lax.all_gather(scaled, 'c', axis=0, tiled=True)  17.2 us
    all_to_all x1, starting transfers between devices, sum_shares(): return lax.all_to_all(mine, 'z', 0, 0)  16.5 us
    all_to_all x1, blocking collectives, sum_shares(): mine = jnp.sum(lax.all_to_all(stacked, PLANE, 0, 0), axis=0)  13.2 us
    all_to_all x1, starting transfers between devices, column_of_weights(): lax.all_to_all(jnp.broadcast_to(piece[None], (depth, HIGH, WIDE)), 'z', 0...  12.8 us
    all_to_all x1, waiting for transfers between devices, column_of_weights(): lax.all_to_all(jnp.broadcast_to(piece[None], (depth, HIGH, WIDE)), 'z', 0...  9.61 us
    ppermute x2, starting transfers between devices, exchange_rims(): lax.ppermute(tail, TILE, [(i, i + 1) for i in range(ends)])  8.37 us
    ppermute x2, starting transfers between devices, exchange_rims(): lax.ppermute(head, TILE, [(i + 1, i) for i in range(ends)])  8.26 us
    all_to_all x1, starting transfers between devices, gather_sums(): lax.all_to_all(jnp.broadcast_to(mine[None], (plane, *mine.shape)), PLANE,...  7.31 us
  transfers between devices with their start and end apart: 15, of which 5 were waited for; matrix products, arithmetic and copies ran while one was open for 11% of the time, Pallas kernels for 2%

profile of v1, /device:TPU:1, one launch (start us, length us, event | category | flops | bytes accessed | tf_op | source)
XLA Modules:
  0.0 189.4 jit_solution(2354481578590136229)
XLA Ops:
  1.8 4.9 %collective-permute-start = (bf16[1,3,64,768]{3,2,1,0:T(8,128)(2,1)S(1)}, bf16[1,3,64,768]{3,2,1,0:T(8,128)(2,1)S(1)}, u32[]{:S(2)}, u32[]{:S(2)}) collective-permute-start(bf16[1,3,64,768]{3,2,1,0:T(8,128)(2,1)S(1)} %get-tuple-element.141), channel_id=1, source_target_pairs={{0,1},{1,2},{2,3},{3,4},{4,5},{5,6},{6,7},{7,8},{8,9},{9,10},{10,1... | collective-permute-start | bytes 884744 | tf_op jit(solution)/shard_map/ppermute | solution.py:24
  6.7 5.1 %collective-permute-start.1 = (bf16[1,3,64,768]{3,2,1,0:T(8,128)(2,1)S(1)}, bf16[1,3,64,768]{3,2,1,0:T(8,128)(2,1)S(1)}, u32[]{:S(2)}, u32[]{:S(2)}) collective-permute-start(bf16[1,3,64,768]{3,2,1,0:T(8,128)(2,1)S(1)} %get-tuple-element.142), channel_id=1, source_target_pairs={{1,0},{2,1},{3,2},{4,3},{5,4},{6,5},{7,6},{8,7},{9,8},{10,9},{11,1... | collective-permute-start | bytes 884744 | tf_op jit(solution)/shard_map/ppermute | solution.py:25
  13.0 2.0 %all-gather.1 = bf16[2,12,768]{2,1,0:T(8,128)(2,1)S(1)} all-gather(bf16[1,12,768]{2,1,0:T(8,128)(2,1)S(1)} %fusion.30), channel_id=2, replica_groups=mesh['yh'=2,'x'=4,'yl'=2,'z'=16,'c'=2] {'c'}, dimensions={0}, use_global_device_ids=true | all-gather | bytes 55296 | tf_op jit(solution)/shard_map/all_gather | solution.py:98
  16.5 12.8 %all-to-all-start = ((bf16[16,24,384]{2,1,0:T(8,128)(2,1)}), bf16[16,24,384]{2,1,0:T(8,128)(2,1)}, u32[]{:S(2)}, u32[]{:S(2)}) async-start(bf16[16,24,384]{2,1,0:T(8,128)(2,1)} %broadcast_in_dim.10), calls=%async_computation | async-start | bytes 589824 | tf_op jit(solution)/shard_map/all_to_all | solution.py:105
  32.7 1.4 fusion.37
  34.2 9.6 %all-to-all-done = bf16[16,24,384]{2,1,0:T(8,128)(2,1)} async-done(((bf16[16,24,384]{2,1,0:T(8,128)(2,1)}), bf16[16,24,384]{2,1,0:T(8,128)(2,1)}, u32[]{:S(2)}, u32[]{:S(2)}) %all-to-all-start) | async-done | bytes 294944 | tf_op jit(solution)/shard_map/all_to_all | solution.py:105
  43.8 2.1 %broadcast_in_dim.11 = bf16[4,16,24,384]{3,2,1,0:T(8,128)(2,1)} broadcast(bf16[16,24,384]{2,1,0:T(8,128)(2,1)} %all-to-all-done), dimensions={1,2,3} | broadcast | bytes 1474560 | tf_op jit(solution)/shard_map/broadcast_in_dim | solution.py:110
  45.9 4.3 %all-to-all-start.1 = ((bf16[4,16,24,384]{3,2,1,0:T(8,128)(2,1)}), bf16[4,16,24,384]{3,2,1,0:T(8,128)(2,1)}, u32[]{:S(2)}, u32[]{:S(2)}) async-start(bf16[4,16,24,384]{3,2,1,0:T(8,128)(2,1)} %broadcast_in_dim.11), calls=%async_computation.1 | async-start | bytes 2359296 | tf_op jit(solution)/shard_map/all_to_all | solution.py:110
  50.3 6.5 %fusion.162 = (f32[4,64]{1,0:T(4,128)S(1)}, f32[1,4,64,768]{3,2,1,0:T(8,128)S(1)}) fusion(bf16[1,10,70,768]{3,2,1,0:T(8,128)(2,1)S(1)} %fusion.37, f32[768]{0:T(1024)S(1)} %get-tuple-element.82, f32[768]{0:T(1024)S(1)} %get-tuple-element.129, f32[768]{0:T(1024)S(1)} %get-tuple-element.130, ...), kind=kLoop, calls=%fused_computation.352 | loop fusion | flops 28901120 | bytes 20205568 | tf_op jit(solution)/shard_map/reduce_sum | solution.py:260
  58.1 2.6 %all-to-all-done.1 = bf16[4,16,24,384]{3,2,1,0:T(8,128)(2,1)} async-done(((bf16[4,16,24,384]{3,2,1,0:T(8,128)(2,1)}), bf16[4,16,24,384]{3,2,1,0:T(8,128)(2,1)}, u32[]{:S(2)}, u32[]{:S(2)}) %all-to-all-start.1) | async-done | bytes 1179680 | tf_op jit(solution)/shard_map/all_to_all | solution.py:110
  62.0 3.1 %collective-permute-start.3 = (bf16[768,384]{1,0:T(8,128)(2,1)S(1)}, bf16[768,384]{1,0:T(8,128)(2,1)}, u32[]{:S(2)}, u32[]{:S(2)}) collective-permute-start(bf16[768,384]{1,0:T(8,128)(2,1)S(1)} %get-tuple-element.136.e0), channel_id=1, source_target_pairs={{0,64},{64,0},{128,192},{192,128},{1,65},{65,1},{129,193},{193,129... | collective-permute-start | bytes 1769480 | tf_op jit(solution)/shard_map/ppermute | solution.py:114
  65.2 3.7 %collective-permute-start.5 = (bf16[768,384]{1,0:T(8,128)(2,1)S(1)}, bf16[768,384]{1,0:T(8,128)(2,1)S(1)}, u32[]{:S(2)}, u32[]{:S(2)}) collective-permute-start(bf16[768,384]{1,0:T(8,128)(2,1)S(1)} %get-tuple-element.135.r0), channel_id=1, source_target_pairs={{0,192},{192,0},{64,128},{128,64},{1,193},{193,1},{65,129},{129,65... | collective-permute-start | bytes 1769480 | tf_op jit(solution)/shard_map/ppermute | solution.py:115
  68.9 2.2 %collective-permute-start.7 = (bf16[768,384]{1,0:T(8,128)(2,1)S(1)}, bf16[768,384]{1,0:T(8,128)(2,1)}, u32[]{:S(2)}, u32[]{:S(2)}) collective-permute-start(bf16[768,384]{1,0:T(8,128)(2,1)S(1)} %get-tuple-element.135.r0), channel_id=1, source_target_pairs={{0,64},{64,0},{128,192},{192,128},{1,65},{65,1},{129,193},{193,129... | collective-permute-start | bytes 1769480 | tf_op jit(solution)/shard_map/ppermute | solution.py:116
  71.1 2.5 %collective-permute-start.2 = (bf16[768,384]{1,0:T(8,128)(2,1)S(1)}, bf16[768,384]{1,0:T(8,128)(2,1)}, u32[]{:S(2)}, u32[]{:S(2)}) collective-permute-start(bf16[768,384]{1,0:T(8,128)(2,1)S(1)} %get-tuple-element.136.e0), channel_id=1, source_target_pairs={{0,192},{192,0},{64,128},{128,64},{1,193},{193,1},{65,129},{129,65... | collective-permute-start | bytes 1769480 | tf_op jit(solution)/shard_map/ppermute | solution.py:117
  73.7 4.0 %collective-permute-start.4 = (bf16[768,384]{1,0:T(8,128)(2,1)}, bf16[768,384]{1,0:T(8,128)(2,1)}, u32[]{:S(2)}, u32[]{:S(2)}) collective-permute-start(bf16[768,384]{1,0:T(8,128)(2,1)} %collective-permute-done.3.e1), channel_id=1, source_target_pairs={{0,192},{192,0},{64,128},{128,64},{1,193},{193,1},{65,129},{129,65... | collective-permute-start | bytes 1769480 | tf_op jit(solution)/shard_map/ppermute | solution.py:118
  77.7 1.9 %collective-permute-start.6 = (bf16[768,384]{1,0:T(8,128)(2,1)S(1)}, bf16[768,384]{1,0:T(8,128)(2,1)}, u32[]{:S(2)}, u32[]{:S(2)}) collective-permute-start(bf16[768,384]{1,0:T(8,128)(2,1)S(1)} %collective-permute-done.5.r0), channel_id=1, source_target_pairs={{0,64},{64,0},{128,192},{192,128},{1,65},{65,1},{129,193},{193,129... | collective-permute-start | bytes 1769480 | tf_op jit(solution)/shard_map/ppermute | solution.py:119
  79.9 17.2 %all_gather.14.scaled_ref = bf16[512,768]{1,0:T(8,128)(2,1)S(1)} all-gather(bf16[256,768]{1,0:T(8,128)(2,1)} %bitcast.92), channel_id=1, replica_groups=mesh['yh'=2,'x'=4,'yl'=2,'z'=16,'c'=2] {'c'}, dimensions={0}, use_global_device_ids=true | all-gather | bytes 1179648 | tf_op jit(solution)/shard_map/all_gather | solution.py:120
  97.2 2.7 %all_gather.15.masked_ref = bf16[512,768]{1,0:T(8,128)(2,1)S(1)} all-gather(bf16[256,768]{1,0:T(8,128)(2,1)} %bitcast.91), channel_id=1, replica_groups=mesh['yh'=2,'x'=4,'yl'=2,'z'=16,'c'=2] {'c'}, dimensions={0}, use_global_device_ids=true | all-gather | bytes 1179648 | tf_op jit(solution)/shard_map/all_gather | solution.py:121
  99.9 4.5 %pointwise_first.1 = (f32[512,768]{1,0:T(8,128)S(1)}, f32[8,1,384]{2,1,0:T(1,128)S(1)}) custom-call(s32[2]{0:T(128)S(1)} %pad_add_fusion.where_ref, bf16[512,768]{1,0:T(8,128)(2,1)S(1)} %all_gather.14.scaled_ref, bf16[512,768]{1,0:T(8,128)(2,1)S(1)} %all_gather.15.masked_ref, f32[8,1,384]{2,1,0:T(1,128)S(1)} %reshape.425.bias_ref, ...), custom_call_target="tpu_custom_call" | custom-call | flops 1811939328 | bytes 20971520 | tf_op jit(solution)/shard_map/pointwise_first/pallas_call | solution.py:208
  105.5 5.7 %pointwise_second.1 = (f32[256,768]{1,0:T(8,128)S(1)}, f32[256,768]{1,0:T(8,128)}, f32[8,1,384]{2,1,0:T(1,128)S(1)}) custom-call(s32[2]{0:T(128)S(1)} %pad_add_fusion.where_ref, bf16[512,768]{1,0:T(8,128)(2,1)S(1)} %all_gather.14.scaled_ref, bf16[512,768]{1,0:T(8,128)(2,1)S(1)} %all_gather.15.masked_ref, f32[8,1,384]{2,1,0:T(1,128)S(1)} %reshape.425.bias_ref, ...), custom_call_target="tpu_custom_call" | custom-call | flops 1811939328 | bytes 20971520 | tf_op jit(solution)/shard_map/pointwise_second/pallas_call | solution.py:217
  111.2 6.8 %collective-permute-start.8 = (f32[256,768]{1,0:T(8,128)}, f32[256,768]{1,0:T(8,128)S(1)}, u32[]{:S(2)}, u32[]{:S(2)}) collective-permute-start(f32[256,768]{1,0:T(8,128)} %get-tuple-element.20), channel_id=1, source_target_pairs={{0,1},{1,0},{2,3},{3,2},{4,5},{5,4},{6,7},{7,6},{8,9},{9,8},{10,11... | collective-permute-start | bytes 2359304 | tf_op jit(solution)/shard_map/ppermute | solution.py:227
  118.3 1.8 collective-permute-done.8.other_ref
  121.2 1.9 %fusion.144 = (f32[768]{0:T(1024)S(1)}, f32[768]{0:T(1024)S(1)}, f32[768]{0:T(1024)S(1)}, f32[768]{0:T(1024)S(1)}, f32[768]{0:T(1024)S(1)}, /*index=5*/f32[768]{...) fusion(bf16[1,10,70,768]{3,2,1,0:T(8,128)(2,1)S(1)} %copy-done., ...), kind=kLoop, calls=%fused_computation.250 | loop fusion | flops 10799616 | bytes 7526400 | tf_op jit(solution)/shard_map/reduce_sum | solution.py:290
  124.3 1.9 %fusion.123 = (f32[768]{0:T(1024)S(1)}, f32[768]{0:T(1024)S(1)}, f32[768]{0:T(1024)S(1)}, f32[768]{0:T(1024)S(1)}, f32[768]{0:T(1024)S(1)}, /*index=5*/f32[768]{...) fusion(bf16[1,10,70,768]{3,2,1,0:T(8,128)(2,1)S(1)} %copy-done., ...), kind=kLoop, calls=%fused_computation.229 | loop fusion | flops 10799616 | bytes 7526400 | tf_op jit(solution)/shard_map/reduce_sum | solution.py:290
  127.5 13.2 %all_to_all.25 = f32[32,16,128]{2,1,0:T(8,128)S(1)} all-to-all(f32[32,16,128]{2,1,0:T(8,128)S(1)} %bitcast.93), channel_id=1, replica_groups=mesh['yh'=2,'x'=4,'yl'=2,'z'=16,'c'=2] {'yh','x','yl','c'}, dimensions={0} | all-to-all | bytes 524288 | tf_op jit(solution)/shard_map/all_to_all | solution.py:64
  141.4 16.5 %all-to-all-start.3 = ((f32[16,16,128]{2,1,0:T(8,128)}), f32[16,16,128]{2,1,0:T(8,128)S(1)}, u32[]{:S(2)}, u32[]{:S(2)}) async-start(f32[16,16,128]{2,1,0:T(8,128)} %broadcast_in_dim.13), calls=%async_computation.3 | async-start | bytes 262144 | tf_op jit(solution)/shard_map/all_to_all | solution.py:66
  158.2 3.1 %collective-permute-start.10 = (bf16[1,3,64,768]{3,2,1,0:T(8,128)(2,1)S(1)}, bf16[1,3,64,768]{3,2,1,0:T(8,128)(2,1)S(1)}, u32[]{:S(2)}, u32[]{:S(2)}) collective-permute-start(bf16[1,3,64,768]{3,2,1,0:T(8,128)(2,1)S(1)} %get-tuple-element.138), channel_id=1, source_target_pairs={{1,0},{2,1},{3,2},{4,3},{5,4},{6,5},{7,6},{8,7},{9,8},{10,9},{11,1... | collective-permute-start | bytes 884744 | tf_op jit(solution)/shard_map/ppermute | solution.py:25
  161.4 3.4 %collective-permute-start.9 = (bf16[1,3,64,768]{3,2,1,0:T(8,128)(2,1)S(1)}, bf16[1,3,64,768]{3,2,1,0:T(8,128)(2,1)S(1)}, u32[]{:S(2)}, u32[]{:S(2)}) collective-permute-start(bf16[1,3,64,768]{3,2,1,0:T(8,128)(2,1)S(1)} %get-tuple-element.137), channel_id=1, source_target_pairs={{0,1},{1,2},{2,3},{3,4},{4,5},{5,6},{6,7},{7,8},{8,9},{9,10},{10,1... | collective-permute-start | bytes 884744 | tf_op jit(solution)/shard_map/ppermute | solution.py:24
  164.8 5.2 %collective-permute-done.10 = bf16[1,3,64,768]{3,2,1,0:T(8,128)(2,1)S(1)} collective-permute-done((bf16[1,3,64,768]{3,2,1,0:T(8,128)(2,1)S(1)}, bf16[1,3,64,768]{3,2,1,0:T(8,128)(2,1)S(1)}, u32[]{:S(2)}, u32[]{:S(2)}) %collective-permute-start.10) | collective-permute-done | bytes 294944 | tf_op jit(solution)/shard_map/ppermute | solution.py:25
  171.1 7.3 %all-to-all-start.4 = ((f32[32,16,128]{2,1,0:T(8,128)}), f32[32,16,128]{2,1,0:T(8,128)S(1)}, u32[]{:S(2)}, u32[]{:S(2)}) async-start(f32[32,16,128]{2,1,0:T(8,128)} %broadcast_in_dim.14), calls=%async_computation.4 | async-start | bytes 524288 | tf_op jit(solution)/shard_map/all_to_all | solution.py:72
  178.6 6.5 %fusion.95 = bf16[1,4,64,768]{3,2,1,0:T(8,128)(2,1)} fusion(bf16[1,4,64,768]{3,2,1,0:T(8,128)(2,1)S(1)} %bitcast.88, bf16[1,4,64,768]{3,2,1,0:T(8,128)(2,1)S(1)} %copy-done.11, bf16[1,3,64,768]{3,2,1,0:T(8,128)(2,1)S(1)} %collective-permute-done.10, bf16[1,3,64,768]{3,2,1,0:T(8,128)(2,1)S(1)} %collective-permute-done.9, ...), kind=kLoop, calls=%fused_computation.201 | loop fusion | flops 30474240 | bytes 18435072 | tf_op jit(solution)/shard_map/convert_element_type | solution.py:303
  185.2 2.0 %all-to-all-done.4 = f32[32,16,128]{2,1,0:T(8,128)S(1)} async-done(((f32[32,16,128]{2,1,0:T(8,128)}), f32[32,16,128]{2,1,0:T(8,128)S(1)}, u32[]{:S(2)}, u32[]{:S(2)}) %all-to-all-start.4) | async-done | bytes 262176 | tf_op jit(solution)/shard_map/all_to_all | solution.py:72
  (259 shorter events, 17.9 us)
Async XLA Ops:
  1.8 29.2 %collective-permute-start = (bf16[1,3,64,768]{3,2,1,0:T(8,128)(2,1)S(1)}, bf16[1,3,64,768]{3,2,1,0:T(8,128)(2,1)S(1)}, u32[]{:S(2)}, u32[]{:S(2)}) collective-permute-start(bf16[1,3,64,768]{3,2,1,0:T(8,128)(2,1)S(1)} %get-tuple-element.141), channel_id=1, source_target_pairs={{0,1},{1,2},{2,3},{3,4},{4,5},{5,6},{6,7},{7,8},{8,9},{9,10},{10,1... | collective-permute-start | bytes 884744 | tf_op jit(solution)/shard_map/ppermute | solution.py:24
  6.7 25.1 %collective-permute-start.1 = (bf16[1,3,64,768]{3,2,1,0:T(8,128)(2,1)S(1)}, bf16[1,3,64,768]{3,2,1,0:T(8,128)(2,1)S(1)}, u32[]{:S(2)}, u32[]{:S(2)}) collective-permute-start(bf16[1,3,64,768]{3,2,1,0:T(8,128)(2,1)S(1)} %get-tuple-element.142), channel_id=1, source_target_pairs={{1,0},{2,1},{3,2},{4,3},{5,4},{6,5},{7,6},{8,7},{9,8},{10,9},{11,1... | collective-permute-start | bytes 884744 | tf_op jit(solution)/shard_map/ppermute | solution.py:25
  16.5 27.2 %all-to-all-start = ((bf16[16,24,384]{2,1,0:T(8,128)(2,1)}), bf16[16,24,384]{2,1,0:T(8,128)(2,1)}, u32[]{:S(2)}, u32[]{:S(2)}) async-start(bf16[16,24,384]{2,1,0:T(8,128)(2,1)} %broadcast_in_dim.10), calls=%async_computation | async-start | bytes 589824 | tf_op jit(solution)/shard_map/all_to_all | solution.py:105
  30.8 26.0 %copy-start.44 = (f32[768]{0:T(1024)}, f32[768]{0:T(1024)S(1)}, u32[]{:S(2)}) copy-start(f32[768]{0:T(1024)S(1)} %get-tuple-element.120) | copy-start | bytes 9220
  30.8 26.0 %copy-start.46 = (f32[768]{0:T(1024)}, f32[768]{0:T(1024)S(1)}, u32[]{:S(2)}) copy-start(f32[768]{0:T(1024)S(1)} %get-tuple-element.121) | copy-start | bytes 9220
  30.8 26.0 %copy-start.48 = (f32[768]{0:T(1024)}, f32[768]{0:T(1024)S(1)}, u32[]{:S(2)}) copy-start(f32[768]{0:T(1024)S(1)} %get-tuple-element.122) | copy-start | bytes 9220
  30.9 26.0 %copy-start.50 = (f32[768]{0:T(1024)}, f32[768]{0:T(1024)S(1)}, u32[]{:S(2)}) copy-start(f32[768]{0:T(1024)S(1)} %get-tuple-element.123) | copy-start | bytes 9220
  30.9 26.0 %copy-start.52 = (f32[768]{0:T(1024)}, f32[768]{0:T(1024)S(1)}, u32[]{:S(2)}) copy-start(f32[768]{0:T(1024)S(1)} %get-tuple-element.124) | copy-start | bytes 9220
  30.9 26.0 %copy-start.54 = (f32[768]{0:T(1024)}, f32[768]{0:T(1024)S(1)}, u32[]{:S(2)}) copy-start(f32[768]{0:T(1024)S(1)} %get-tuple-element.125) | copy-start | bytes 9220
  30.9 26.0 %copy-start.56 = (f32[768]{0:T(1024)}, f32[768]{0:T(1024)S(1)}, u32[]{:S(2)}) copy-start(f32[768]{0:T(1024)S(1)} %get-tuple-element.126) | copy-start | bytes 9220
  30.9 26.0 %copy-start.58 = (f32[768]{0:T(1024)}, f32[768]{0:T(1024)S(1)}, u32[]{:S(2)}) copy-start(f32[768]{0:T(1024)S(1)} %get-tuple-element.127) | copy-start | bytes 9220
  30.9 26.0 %copy-start.60 = (f32[768]{0:T(1024)}, f32[768]{0:T(1024)S(1)}, u32[]{:S(2)}) copy-start(f32[768]{0:T(1024)S(1)} %get-tuple-element.128) | copy-start | bytes 9220
  30.9 26.0 %copy-start.62 = (f32[768]{0:T(1024)}, f32[768]{0:T(1024)S(1)}, u32[]{:S(2)}) copy-start(f32[768]{0:T(1024)S(1)} %get-tuple-element.129) | copy-start | bytes 9220
  30.9 26.0 %copy-start.64 = (f32[768]{0:T(1024)}, f32[768]{0:T(1024)S(1)}, u32[]{:S(2)}) copy-start(f32[768]{0:T(1024)S(1)} %get-tuple-element.130) | copy-start | bytes 9220
  45.9 14.8 %all-to-all-start.1 = ((bf16[4,16,24,384]{3,2,1,0:T(8,128)(2,1)}), bf16[4,16,24,384]{3,2,1,0:T(8,128)(2,1)}, u32[]{:S(2)}, u32[]{:S(2)}) async-start(bf16[4,16,24,384]{3,2,1,0:T(8,128)(2,1)} %broadcast_in_dim.11), calls=%async_computation.1 | async-start | bytes 2359296 | tf_op jit(solution)/shard_map/all_to_all | solution.py:110
  58.1 21.6 %copy-start.67 = (f32[3072]{0:T(1024)S(1)}, f32[3072]{0:T(1024)}, u32[]{:S(2)}) copy-start(f32[3072]{0:T(1024)} %param.13) | copy-start | bytes 36868
  62.0 11.6 %collective-permute-start.3 = (bf16[768,384]{1,0:T(8,128)(2,1)S(1)}, bf16[768,384]{1,0:T(8,128)(2,1)}, u32[]{:S(2)}, u32[]{:S(2)}) collective-permute-start(bf16[768,384]{1,0:T(8,128)(2,1)S(1)} %get-tuple-element.136.e0), channel_id=1, source_target_pairs={{0,64},{64,0},{128,192},{192,128},{1,65},{65,1},{129,193},{193,129... | collective-permute-start | bytes 1769480 | tf_op jit(solution)/shard_map/ppermute | solution.py:114
  65.2 12.5 %collective-permute-start.5 = (bf16[768,384]{1,0:T(8,128)(2,1)S(1)}, bf16[768,384]{1,0:T(8,128)(2,1)S(1)}, u32[]{:S(2)}, u32[]{:S(2)}) collective-permute-start(bf16[768,384]{1,0:T(8,128)(2,1)S(1)} %get-tuple-element.135.r0), channel_id=1, source_target_pairs={{0,192},{192,0},{64,128},{128,64},{1,193},{193,1},{65,129},{129,65... | collective-permute-start | bytes 1769480 | tf_op jit(solution)/shard_map/ppermute | solution.py:115
  68.9 31.0 %collective-permute-start.7 = (bf16[768,384]{1,0:T(8,128)(2,1)S(1)}, bf16[768,384]{1,0:T(8,128)(2,1)}, u32[]{:S(2)}, u32[]{:S(2)}) collective-permute-start(bf16[768,384]{1,0:T(8,128)(2,1)S(1)} %get-tuple-element.135.r0), channel_id=1, source_target_pairs={{0,64},{64,0},{128,192},{192,128},{1,65},{65,1},{129,193},{193,129... | collective-permute-start | bytes 1769480 | tf_op jit(solution)/shard_map/ppermute | solution.py:116
  71.1 33.3 %collective-permute-start.2 = (bf16[768,384]{1,0:T(8,128)(2,1)S(1)}, bf16[768,384]{1,0:T(8,128)(2,1)}, u32[]{:S(2)}, u32[]{:S(2)}) collective-permute-start(bf16[768,384]{1,0:T(8,128)(2,1)S(1)} %get-tuple-element.136.e0), channel_id=1, source_target_pairs={{0,192},{192,0},{64,128},{128,64},{1,193},{193,1},{65,129},{129,65... | collective-permute-start | bytes 1769480 | tf_op jit(solution)/shard_map/ppermute | solution.py:117
  73.7 30.8 %collective-permute-start.4 = (bf16[768,384]{1,0:T(8,128)(2,1)}, bf16[768,384]{1,0:T(8,128)(2,1)}, u32[]{:S(2)}, u32[]{:S(2)}) collective-permute-start(bf16[768,384]{1,0:T(8,128)(2,1)} %collective-permute-done.3.e1), channel_id=1, source_target_pairs={{0,192},{192,0},{64,128},{128,64},{1,193},{193,1},{65,129},{129,65... | collective-permute-start | bytes 1769480 | tf_op jit(solution)/shard_map/ppermute | solution.py:118
  77.6 26.8 %copy-start.1 = (bf16[768,384]{1,0:T(8,128)(2,1)}, bf16[768,384]{1,0:T(8,128)(2,1)S(1)}, u32[]{:S(2)}) copy-start(bf16[768,384]{1,0:T(8,128)(2,1)S(1)} %collective-permute-done.5.r0) | copy-start | bytes 1769476
  77.7 26.8 %collective-permute-start.6 = (bf16[768,384]{1,0:T(8,128)(2,1)S(1)}, bf16[768,384]{1,0:T(8,128)(2,1)}, u32[]{:S(2)}, u32[]{:S(2)}) collective-permute-start(bf16[768,384]{1,0:T(8,128)(2,1)S(1)} %collective-permute-done.5.r0), channel_id=1, source_target_pairs={{0,64},{64,0},{128,192},{192,128},{1,65},{65,1},{129,193},{193,129... | collective-permute-start | bytes 1769480 | tf_op jit(solution)/shard_map/ppermute | solution.py:119
  111.2 8.9 %collective-permute-start.8 = (f32[256,768]{1,0:T(8,128)}, f32[256,768]{1,0:T(8,128)S(1)}, u32[]{:S(2)}, u32[]{:S(2)}) collective-permute-start(f32[256,768]{1,0:T(8,128)} %get-tuple-element.20), channel_id=1, source_target_pairs={{0,1},{1,0},{2,3},{3,2},{4,5},{5,4},{6,7},{7,6},{8,9},{9,8},{10,11... | collective-permute-start | bytes 2359304 | tf_op jit(solution)/shard_map/ppermute | solution.py:227
  141.4 28.9 %all-to-all-start.3 = ((f32[16,16,128]{2,1,0:T(8,128)}), f32[16,16,128]{2,1,0:T(8,128)S(1)}, u32[]{:S(2)}, u32[]{:S(2)}) async-start(f32[16,16,128]{2,1,0:T(8,128)} %broadcast_in_dim.13), calls=%async_computation.3 | async-start | bytes 262144 | tf_op jit(solution)/shard_map/all_to_all | solution.py:66
  158.0 20.4 %copy-start.11 = (bf16[1,4,64,768]{3,2,1,0:T(8,128)(2,1)S(1)}, bf16[1,4,64,768]{3,2,1,0:T(8,128)(2,1)}, u32[]{:S(2)}) copy-start(bf16[1,4,64,768]{3,2,1,0:T(8,128)(2,1)} %param.9) | copy-start | bytes 1179652
  158.0 20.4 %copy-start.17 = (f32[768]{0:T(1024)S(1)}, f32[768]{0:T(1024)}, u32[]{:S(2)}) copy-start(f32[768]{0:T(1024)} %copy-done.16) | copy-start | bytes 9220
  158.0 20.4 %copy-start.19 = (f32[768]{0:T(1024)S(1)}, f32[768]{0:T(1024)}, u32[]{:S(2)}) copy-start(f32[768]{0:T(1024)} %copy-done.18) | copy-start | bytes 9220
  158.0 20.4 %copy-start.21 = (f32[768]{0:T(1024)S(1)}, f32[768]{0:T(1024)}, u32[]{:S(2)}) copy-start(f32[768]{0:T(1024)} %copy-done.20) | copy-start | bytes 9220
  158.2 11.8 %collective-permute-start.10 = (bf16[1,3,64,768]{3,2,1,0:T(8,128)(2,1)S(1)}, bf16[1,3,64,768]{3,2,1,0:T(8,128)(2,1)S(1)}, u32[]{:S(2)}, u32[]{:S(2)}) collective-permute-start(bf16[1,3,64,768]{3,2,1,0:T(8,128)(2,1)S(1)} %get-tuple-element.138), channel_id=1, source_target_pairs={{1,0},{2,1},{3,2},{4,3},{5,4},{6,5},{7,6},{8,7},{9,8},{10,9},{11,1... | collective-permute-start | bytes 884744 | tf_op jit(solution)/shard_map/ppermute | solution.py:25
  161.4 8.6 %collective-permute-start.9 = (bf16[1,3,64,768]{3,2,1,0:T(8,128)(2,1)S(1)}, bf16[1,3,64,768]{3,2,1,0:T(8,128)(2,1)S(1)}, u32[]{:S(2)}, u32[]{:S(2)}) collective-permute-start(bf16[1,3,64,768]{3,2,1,0:T(8,128)(2,1)S(1)} %get-tuple-element.137), channel_id=1, source_target_pairs={{0,1},{1,2},{2,3},{3,4},{4,5},{5,6},{6,7},{7,8},{8,9},{9,10},{10,1... | collective-permute-start | bytes 884744 | tf_op jit(solution)/shard_map/ppermute | solution.py:24
  171.1 16.1 %all-to-all-start.4 = ((f32[32,16,128]{2,1,0:T(8,128)}), f32[32,16,128]{2,1,0:T(8,128)S(1)}, u32[]{:S(2)}, u32[]{:S(2)}) async-start(f32[32,16,128]{2,1,0:T(8,128)} %broadcast_in_dim.14), calls=%async_computation.4 | async-start | bytes 524288 | tf_op jit(solution)/shard_map/all_to_all | solution.py:72
  (52 other events, 874.6 us)

commit v2 on v1

--- a/solution.py
+++ b/solution.py
@@ -124,24 +124,28 @@
     return first, second, scaled, masked
 
 
-def add_band(band, first_side, scaled_ref, masked_ref, bias_ref, expand, reduce, bias_out, total):
+def add_band(band, first_side, cells, scaled_ref, masked_ref, bias_ref, expand, reduce, waits, bias_out, total):
     contract_last = (((1,), (1,)), ((), ()))
     sides = (first_side, 1 - first_side)
     for part in range(2):
         half = pl.ds(pl.multiple_of(sides[part] * WIDE, WIDE), WIDE)
-        hidden = jnp.dot(scaled_ref[...], expand[part][...], preferred_element_type=jnp.float32)
+        if waits:
+            waits[3 if part else 0].wait()
+        hidden = jnp.dot(scaled_ref[cells, :], expand[part][...], preferred_element_type=jnp.float32)
         slope = gelu_slope(hidden + bias_ref[band * 2 + sides[part]])
         back_act = None
         for other in range(2):
+            if waits and not part:
+                waits[1 + other].wait()
             term = lax.dot_general(
-                masked_ref[:, pl.ds(pl.multiple_of(sides[other] * WIDE, WIDE), WIDE)],
+                masked_ref[cells, pl.ds(pl.multiple_of(sides[other] * WIDE, WIDE), WIDE)],
                 reduce[other][half, :],
                 contract_last,
                 preferred_element_type=jnp.float32,
             )
             back_act = term if back_act is None else back_act + term
         back_hidden = (back_act * slope).astype(jnp.bfloat16)
-        bias_out[band * 2 + sides[part]] = jnp.sum(back_hidden.astype(jnp.float32), axis=0, keepdims=True)
+        bias_out[band * 2 + sides[part]] += jnp.sum(back_hidden.astype(jnp.float32), axis=0, keepdims=True)
         total[...] += lax.dot_general(
             back_hidden, expand[part][...], contract_last, preferred_element_type=jnp.float32
         )
@@ -152,22 +156,30 @@
     bias_out[...] = jnp.zeros_like(bias_out)
     total_ref[...] = jnp.zeros_like(total_ref)
     add_band(
-        2 * core + lax.div(column, 2), lax.rem(column, 2), scaled_ref, masked_ref, bias_ref,
-        (e0, e1), (r0, r1), bias_out, total_ref,
+        2 * core + lax.div(column, 2), lax.rem(column, 2), slice(None), scaled_ref, masked_ref, bias_ref,
+        (e0, e1), (r0, r1), (), bias_out, total_ref,
     )
 
 
 def second_body(
-    where_ref, scaled_ref, masked_ref, bias_ref, e0, e1, r0, r1, sum_ref, bias_in,
-    mine_ref, other_ref, bias_out, total,
+    where_ref, scaled_ref, masked_ref, bias_ref, e0, r0, e1, r1, sum_ref, bias_in,
+    mine_ref, other_ref, bias_out, total, expand, reduce, sems,
 ):
+    waits = (
+        pltpu.make_async_copy(e0, expand.at[0], sems.at[0]),
+        pltpu.make_async_copy(r0, reduce.at[0], sems.at[1]),
+        pltpu.make_async_copy(r1, reduce.at[1], sems.at[2]),
+        pltpu.make_async_copy(e1, expand.at[1], sems.at[3]),
+    )
+    for copy in waits:
+        copy.start()
     column, core = where_ref[0], where_ref[1]
     cells = mine_ref.shape[0]
     bias_out[...] = bias_in[...]
     total[...] = sum_ref[...]
     add_band(
-        2 * core + 1 - lax.div(column, 2), 1 - lax.rem(column, 2), scaled_ref, masked_ref, bias_ref,
-        (e0, e1), (r0, r1), bias_out, total,
+        2 * core + 1 - lax.div(column, 2), 1 - lax.rem(column, 2), slice(None), scaled_ref, masked_ref, bias_ref,
+        (expand.at[0], expand.at[1]), (reduce.at[0], reduce.at[1]), waits, bias_out, total,
     )
     mine_ref[...] = total[pl.ds(pl.multiple_of(core * cells, cells), cells), :]
     other_ref[...] = total[pl.ds(pl.multiple_of((1 - core) * cells, cells), cells), :]
@@ -214,16 +226,22 @@
         cost_estimate=cost,
         name="pointwise_first",
     )(where, scaled, masked, bias, *first)
+    far_expand, across_expand, far_reduce, across_reduce = second
     mine, other, bias_part = pl.pallas_call(
         second_body,
         out_shape=(half, half, bias_shape),
-        in_specs=[smem] + [vmem] * 9,
+        in_specs=[smem] + [vmem] * 3 + [pl.BlockSpec(memory_space=pl.ANY)] * 4 + [vmem] * 2,
         out_specs=(vmem, vmem, vmem),
-        scratch_shapes=[pltpu.VMEM((2 * cells, channels), jnp.float32)],
+        scratch_shapes=[
+            pltpu.VMEM((2 * cells, channels), jnp.float32),
+            pltpu.VMEM((2, channels, WIDE), jnp.bfloat16),
+            pltpu.VMEM((2, channels, WIDE), jnp.bfloat16),
+            pltpu.SemaphoreType.DMA((4,)),
+        ],
         compiler_params=params,
         cost_estimate=cost,
         name="pointwise_second",
-    )(where, scaled, masked, bias, *second, total, bias_part)
+    )(where, scaled, masked, bias, far_expand, far_reduce, across_expand, across_reduce, total, bias_part)
     other = lax.ppermute(other, "c", ((0, 1), (1, 0)))
     mixed, gain_part = pl.pallas_call(
         norm_body,
@@ -281,7 +299,7 @@
     )
     back_mixed = back_mixed.reshape(samples, row_count, col_count, channels)
     gain_part = gain_part.reshape(channels)
-    bias_part = bias_part.reshape(-1)
+    bias_part = bias_part.reshape(4, 2, depth, HIGH).transpose(1, 2, 0, 3).reshape(-1)
     mixed_float = back_mixed.astype(jnp.float32)
     kernel_rows = []
     for shift_row in range(KS):
@@ -302,7 +320,6 @@
     through = depthwise(back_padded, depth_kernel[::-1, ::-1], row_count, col_count)
     state_grad = (cotangent.astype(jnp.float32) + through).astype(jnp.bfloat16)
     kernel_grad, gain_grad, bias_grad = gather_sums(shares, parts)
-    bias_grad = bias_grad.reshape(4, 2, depth, HIGH).transpose(1, 2, 0, 3).reshape(-1)
     return (state_grad, kernel_grad, gain_grad, bias_grad)
 
 

time: 190 us -> 190 us (level)
    unnamed x145 -> x123, local copies, waits for them, and re-layouts: 2.97 us -> 0.31 us
  transfers between devices with their start and end apart: 15 -> 15, of which waited for: 5 -> 5; matrix products, arithmetic and copies ran while one was open for 11% -> 13% of each run, Pallas kernels for 2% -> 2%
where the time goes in v2:
time: 190 us; the launch traced here: 189 us
  starting transfers between devices  82 us (43%)
  blocking collectives  35.2 us (19%)
  other arithmetic  22.9 us (12%)
  waiting for transfers between devices  19.7 us (10%)
  local copies, waits for them, and re-layouts  13.6 us (7%)
  Pallas kernels  12.2 us (6%)
  between operations  2.41 us (1%)
    all_gather x1, blocking collectives, sheets_of_weights(): scaled = lax.all_gather(scaled, 'c', axis=0, tiled=True)  17.3 us
    all_to_all x1, starting transfers between devices, sum_shares(): return lax.all_to_all(mine, 'z', 0, 0)  16.5 us
    all_to_all x1, blocking collectives, sum_shares(): mine = jnp.sum(lax.all_to_all(stacked, PLANE, 0, 0), axis=0)  13.2 us
    all_to_all x1, starting transfers between devices, column_of_weights(): lax.all_to_all(jnp.broadcast_to(piece[None], (depth, HIGH, WIDE)), 'z', 0...  12.8 us
    all_to_all x1, waiting for transfers between devices, column_of_weights(): lax.all_to_all(jnp.broadcast_to(piece[None], (depth, HIGH, WIDE)), 'z', 0...  9.09 us
    ppermute x2, starting transfers between devices, exchange_rims(): lax.ppermute(tail, TILE, [(i, i + 1) for i in range(ends)])  8.59 us
    ppermute x2, starting transfers between devices, exchange_rims(): lax.ppermute(head, TILE, [(i + 1, i) for i in range(ends)])  8.26 us
    all_to_all x1, starting transfers between devices, gather_sums(): lax.all_to_all(jnp.broadcast_to(mine[None], (plane, *mine.shape)), PLANE,...  7.26 us
  transfers between devices with their start and end apart: 15, of which 5 were waited for; matrix products, arithmetic and copies ran while one was open for 13% of the time, Pallas kernels for 2%

profile of v2, /device:TPU:1, one launch (start us, length us, event | category | flops | bytes accessed | tf_op | source)
XLA Modules:
  0.0 189.1 jit_solution(1930043515914478882)
XLA Ops:
  1.8 4.9 %collective-permute-start = (bf16[1,3,64,768]{3,2,1,0:T(8,128)(2,1)S(1)}, bf16[1,3,64,768]{3,2,1,0:T(8,128)(2,1)S(1)}, u32[]{:S(2)}, u32[]{:S(2)}) collective-permute-start(bf16[1,3,64,768]{3,2,1,0:T(8,128)(2,1)S(1)} %get-tuple-element.141), channel_id=1, source_target_pairs={{0,1},{1,2},{2,3},{3,4},{4,5},{5,6},{6,7},{7,8},{8,9},{9,10},{10,1... | collective-permute-start | bytes 884744 | tf_op jit(solution)/shard_map/ppermute | solution.py:24
  6.7 5.1 %collective-permute-start.1 = (bf16[1,3,64,768]{3,2,1,0:T(8,128)(2,1)S(1)}, bf16[1,3,64,768]{3,2,1,0:T(8,128)(2,1)}, u32[]{:S(2)}, u32[]{:S(2)}) collective-permute-start(bf16[1,3,64,768]{3,2,1,0:T(8,128)(2,1)S(1)} %get-tuple-element.142), channel_id=1, source_target_pairs={{1,0},{2,1},{3,2},{4,3},{5,4},{6,5},{7,6},{8,7},{9,8},{10,9},{11,1... | collective-permute-start | bytes 884744 | tf_op jit(solution)/shard_map/ppermute | solution.py:25
  13.0 2.0 %all-gather.1 = bf16[2,12,768]{2,1,0:T(8,128)(2,1)S(1)} all-gather(bf16[1,12,768]{2,1,0:T(8,128)(2,1)S(1)} %fusion.30), channel_id=2, replica_groups=mesh['yh'=2,'x'=4,'yl'=2,'z'=16,'c'=2] {'c'}, dimensions={0}, use_global_device_ids=true | all-gather | bytes 55296 | tf_op jit(solution)/shard_map/all_gather | solution.py:98
  16.5 12.8 %all-to-all-start = ((bf16[16,24,384]{2,1,0:T(8,128)(2,1)}), bf16[16,24,384]{2,1,0:T(8,128)(2,1)}, u32[]{:S(2)}, u32[]{:S(2)}) async-start(bf16[16,24,384]{2,1,0:T(8,128)(2,1)} %broadcast_in_dim.10), calls=%async_computation | async-start | bytes 589824 | tf_op jit(solution)/shard_map/all_to_all | solution.py:105
  33.2 1.5 fusion.37
  34.7 9.1 %all-to-all-done = bf16[16,24,384]{2,1,0:T(8,128)(2,1)} async-done(((bf16[16,24,384]{2,1,0:T(8,128)(2,1)}), bf16[16,24,384]{2,1,0:T(8,128)(2,1)}, u32[]{:S(2)}, u32[]{:S(2)}) %all-to-all-start) | async-done | bytes 294944 | tf_op jit(solution)/shard_map/all_to_all | solution.py:105
  43.8 2.1 %broadcast_in_dim.11 = bf16[4,16,24,384]{3,2,1,0:T(8,128)(2,1)} broadcast(bf16[16,24,384]{2,1,0:T(8,128)(2,1)} %all-to-all-done), dimensions={1,2,3} | broadcast | bytes 1474560 | tf_op jit(solution)/shard_map/broadcast_in_dim | solution.py:110
  46.0 4.3 %all-to-all-start.1 = ((bf16[4,16,24,384]{3,2,1,0:T(8,128)(2,1)}), bf16[4,16,24,384]{3,2,1,0:T(8,128)(2,1)}, u32[]{:S(2)}, u32[]{:S(2)}) async-start(bf16[4,16,24,384]{3,2,1,0:T(8,128)(2,1)} %broadcast_in_dim.11), calls=%async_computation.1 | async-start | bytes 2359296 | tf_op jit(solution)/shard_map/all_to_all | solution.py:110
  50.6 6.5 %fusion.162 = (f32[4,64]{1,0:T(4,128)S(1)}, f32[1,4,64,768]{3,2,1,0:T(8,128)S(1)}) fusion(bf16[1,10,70,768]{3,2,1,0:T(8,128)(2,1)S(1)} %fusion.37, f32[768]{0:T(1024)S(1)} %get-tuple-element.82, f32[768]{0:T(1024)S(1)} %copy-done.49, f32[768]{0:T(1024)S(1)} %copy-done.51, bf16[1,7,64,768]{3,2,1,0:T(8,128)(2,1)S(1)} %constant_dynamic-update-slice_fusion.2, ...), kind=kLoop, calls=%fused_computation.354 | loop fusion | flops 28901120 | bytes 20205568 | tf_op jit(solution)/shard_map/reduce_sum | solution.py:278
  58.2 2.6 %all-to-all-done.1 = bf16[4,16,24,384]{3,2,1,0:T(8,128)(2,1)} async-done(((bf16[4,16,24,384]{3,2,1,0:T(8,128)(2,1)}), bf16[4,16,24,384]{3,2,1,0:T(8,128)(2,1)}, u32[]{:S(2)}, u32[]{:S(2)}) %all-to-all-start.1) | async-done | bytes 1179680 | tf_op jit(solution)/shard_map/all_to_all | solution.py:110
  60.8 1.4 slice_bitcast_fusion
  62.2 3.1 %collective-permute-start.4 = (bf16[768,384]{1,0:T(8,128)(2,1)S(1)}, bf16[768,384]{1,0:T(8,128)(2,1)}, u32[]{:S(2)}, u32[]{:S(2)}) collective-permute-start(bf16[768,384]{1,0:T(8,128)(2,1)S(1)} %get-tuple-element.136.e0), channel_id=1, source_target_pairs={{0,64},{64,0},{128,192},{192,128},{1,65},{65,1},{129,193},{193,129... | collective-permute-start | bytes 1769480 | tf_op jit(solution)/shard_map/ppermute | solution.py:114
  65.3 3.7 %collective-permute-start.3 = (bf16[768,384]{1,0:T(8,128)(2,1)S(1)}, bf16[768,384]{1,0:T(8,128)(2,1)S(1)}, u32[]{:S(2)}, u32[]{:S(2)}) collective-permute-start(bf16[768,384]{1,0:T(8,128)(2,1)S(1)} %get-tuple-element.135.r0), channel_id=1, source_target_pairs={{0,192},{192,0},{64,128},{128,64},{1,193},{193,1},{65,129},{129,65... | collective-permute-start | bytes 1769480 | tf_op jit(solution)/shard_map/ppermute | solution.py:115
  69.0 2.2 %collective-permute-start.7 = (bf16[768,384]{1,0:T(8,128)(2,1)S(1)}, bf16[768,384]{1,0:T(8,128)(2,1)}, u32[]{:S(2)}, u32[]{:S(2)}) collective-permute-start(bf16[768,384]{1,0:T(8,128)(2,1)S(1)} %get-tuple-element.135.r0), channel_id=1, source_target_pairs={{0,64},{64,0},{128,192},{192,128},{1,65},{65,1},{129,193},{193,129... | collective-permute-start | bytes 1769480 | tf_op jit(solution)/shard_map/ppermute | solution.py:116
  71.3 2.5 %collective-permute-start.2 = (bf16[768,384]{1,0:T(8,128)(2,1)S(1)}, bf16[768,384]{1,0:T(8,128)(2,1)}, u32[]{:S(2)}, u32[]{:S(2)}) collective-permute-start(bf16[768,384]{1,0:T(8,128)(2,1)S(1)} %get-tuple-element.136.e0), channel_id=1, source_target_pairs={{0,192},{192,0},{64,128},{128,64},{1,193},{193,1},{65,129},{129,65... | collective-permute-start | bytes 1769480 | tf_op jit(solution)/shard_map/ppermute | solution.py:117
  73.8 4.0 %collective-permute-start.5 = (bf16[768,384]{1,0:T(8,128)(2,1)}, bf16[768,384]{1,0:T(8,128)(2,1)}, u32[]{:S(2)}, u32[]{:S(2)}) collective-permute-start(bf16[768,384]{1,0:T(8,128)(2,1)} %collective-permute-done.4.e1), channel_id=1, source_target_pairs={{0,192},{192,0},{64,128},{128,64},{1,193},{193,1},{65,129},{129,65... | collective-permute-start | bytes 1769480 | tf_op jit(solution)/shard_map/ppermute | solution.py:118
  77.8 1.9 %collective-permute-start.6 = (bf16[768,384]{1,0:T(8,128)(2,1)S(1)}, bf16[768,384]{1,0:T(8,128)(2,1)}, u32[]{:S(2)}, u32[]{:S(2)}) collective-permute-start(bf16[768,384]{1,0:T(8,128)(2,1)S(1)} %collective-permute-done.3.r0), channel_id=1, source_target_pairs={{0,64},{64,0},{128,192},{192,128},{1,65},{65,1},{129,193},{193,129... | collective-permute-start | bytes 1769480 | tf_op jit(solution)/shard_map/ppermute | solution.py:119
  80.1 17.3 %all_gather.14.scaled_ref = bf16[512,768]{1,0:T(8,128)(2,1)S(1)} all-gather(bf16[256,768]{1,0:T(8,128)(2,1)} %bitcast.94), channel_id=1, replica_groups=mesh['yh'=2,'x'=4,'yl'=2,'z'=16,'c'=2] {'c'}, dimensions={0}, use_global_device_ids=true | all-gather | bytes 1179648 | tf_op jit(solution)/shard_map/all_gather | solution.py:120
  97.3 2.7 %all_gather.15.masked_ref = bf16[512,768]{1,0:T(8,128)(2,1)S(1)} all-gather(bf16[256,768]{1,0:T(8,128)(2,1)} %bitcast.93), channel_id=1, replica_groups=mesh['yh'=2,'x'=4,'yl'=2,'z'=16,'c'=2] {'c'}, dimensions={0}, use_global_device_ids=true | all-gather | bytes 1179648 | tf_op jit(solution)/shard_map/all_gather | solution.py:121
  100.1 4.5 %pointwise_first.1 = (f32[512,768]{1,0:T(8,128)S(1)}, f32[8,1,384]{2,1,0:T(1,128)S(1)}) custom-call(s32[2]{0:T(128)S(1)} %pad_add_fusion.where_ref, bf16[512,768]{1,0:T(8,128)(2,1)S(1)} %all_gather.14.scaled_ref, bf16[512,768]{1,0:T(8,128)(2,1)S(1)} %all_gather.15.masked_ref, f32[8,1,384]{2,1,0:T(1,128)S(1)} %reshape.428.bias_ref, ...), custom_call_target="tpu_custom_call" | custom-call | flops 1811939328 | bytes 20971520 | tf_op jit(solution)/shard_map/pointwise_first/pallas_call | solution.py:220
  104.7 6.6 %pointwise_second.1 = (f32[256,768]{1,0:T(8,128)S(1)}, f32[256,768]{1,0:T(8,128)}, f32[8,1,384]{2,1,0:T(1,128)S(1)}) custom-call(s32[2]{0:T(128)S(1)} %pad_add_fusion.where_ref, bf16[512,768]{1,0:T(8,128)(2,1)S(1)} %all_gather.14.scaled_ref, bf16[512,768]{1,0:T(8,128)(2,1)S(1)} %all_gather.15.masked_ref, f32[8,1,384]{2,1,0:T(1,128)S(1)} %reshape.428.bias_ref, ...), custom_call_target="tpu_custom_call" | custom-call | flops 1811939328 | bytes 20971520 | tf_op jit(solution)/shard_map/pointwise_second/pallas_call | solution.py:230
  111.3 6.8 %collective-permute-start.8 = (f32[256,768]{1,0:T(8,128)}, f32[256,768]{1,0:T(8,128)S(1)}, u32[]{:S(2)}, u32[]{:S(2)}) collective-permute-start(f32[256,768]{1,0:T(8,128)} %get-tuple-element.20), channel_id=1, source_target_pairs={{0,1},{1,0},{2,3},{3,2},{4,5},{5,4},{6,7},{7,6},{8,9},{9,8},{10,11... | collective-permute-start | bytes 2359304 | tf_op jit(solution)/shard_map/ppermute | solution.py:245
  121.2 1.9 %fusion.144 = (f32[768]{0:T(1024)S(1)}, f32[768]{0:T(1024)S(1)}, f32[768]{0:T(1024)S(1)}, f32[768]{0:T(1024)S(1)}, f32[768]{0:T(1024)S(1)}, /*index=5*/f32[768]{...) fusion(bf16[1,10,70,768]{3,2,1,0:T(8,128)(2,1)S(1)} %copy-done., ...), kind=kLoop, calls=%fused_computation.250 | loop fusion | flops 10799616 | bytes 7526400 | tf_op jit(solution)/shard_map/reduce_sum | solution.py:308
  124.4 1.9 %fusion.123 = (f32[768]{0:T(1024)S(1)}, f32[768]{0:T(1024)S(1)}, f32[768]{0:T(1024)S(1)}, f32[768]{0:T(1024)S(1)}, f32[768]{0:T(1024)S(1)}, /*index=5*/f32[768]{...) fusion(bf16[1,10,70,768]{3,2,1,0:T(8,128)(2,1)S(1)} %copy-done., ...), kind=kLoop, calls=%fused_computation.229 | loop fusion | flops 10799616 | bytes 7526400 | tf_op jit(solution)/shard_map/reduce_sum | solution.py:308
  127.5 13.2 %all_to_all.25 = f32[32,16,128]{2,1,0:T(8,128)S(1)} all-to-all(f32[32,16,128]{2,1,0:T(8,128)S(1)} %bitcast.95), channel_id=1, replica_groups=mesh['yh'=2,'x'=4,'yl'=2,'z'=16,'c'=2] {'yh','x','yl','c'}, dimensions={0} | all-to-all | bytes 524288 | tf_op jit(solution)/shard_map/all_to_all | solution.py:64
  141.4 16.5 %all-to-all-start.3 = ((f32[16,16,128]{2,1,0:T(8,128)}), f32[16,16,128]{2,1,0:T(8,128)S(1)}, u32[]{:S(2)}, u32[]{:S(2)}) async-start(f32[16,16,128]{2,1,0:T(8,128)} %broadcast_in_dim.13), calls=%async_computation.3 | async-start | bytes 262144 | tf_op jit(solution)/shard_map/all_to_all | solution.py:66
  158.3 3.1 %collective-permute-start.10 = (bf16[1,3,64,768]{3,2,1,0:T(8,128)(2,1)S(1)}, bf16[1,3,64,768]{3,2,1,0:T(8,128)(2,1)S(1)}, u32[]{:S(2)}, u32[]{:S(2)}) collective-permute-start(bf16[1,3,64,768]{3,2,1,0:T(8,128)(2,1)S(1)} %get-tuple-element.138), channel_id=1, source_target_pairs={{1,0},{2,1},{3,2},{4,3},{5,4},{6,5},{7,6},{8,7},{9,8},{10,9},{11,1... | collective-permute-start | bytes 884744 | tf_op jit(solution)/shard_map/ppermute | solution.py:25
  161.4 3.7 %collective-permute-start.9 = (bf16[1,3,64,768]{3,2,1,0:T(8,128)(2,1)S(1)}, bf16[1,3,64,768]{3,2,1,0:T(8,128)(2,1)S(1)}, u32[]{:S(2)}, u32[]{:S(2)}) collective-permute-start(bf16[1,3,64,768]{3,2,1,0:T(8,128)(2,1)S(1)} %get-tuple-element.137), channel_id=1, source_target_pairs={{0,1},{1,2},{2,3},{3,4},{4,5},{5,6},{6,7},{7,8},{8,9},{9,10},{10,1... | collective-permute-start | bytes 884744 | tf_op jit(solution)/shard_map/ppermute | solution.py:24
  165.1 5.0 %collective-permute-done.10 = bf16[1,3,64,768]{3,2,1,0:T(8,128)(2,1)S(1)} collective-permute-done((bf16[1,3,64,768]{3,2,1,0:T(8,128)(2,1)S(1)}, bf16[1,3,64,768]{3,2,1,0:T(8,128)(2,1)S(1)}, u32[]{:S(2)}, u32[]{:S(2)}) %collective-permute-start.10) | collective-permute-done | bytes 294944 | tf_op jit(solution)/shard_map/ppermute | solution.py:25
  171.1 7.3 %all-to-all-start.4 = ((f32[32,16,128]{2,1,0:T(8,128)}), f32[32,16,128]{2,1,0:T(8,128)S(1)}, u32[]{:S(2)}, u32[]{:S(2)}) async-start(f32[32,16,128]{2,1,0:T(8,128)} %broadcast_in_dim.14), calls=%async_computation.4 | async-start | bytes 524288 | tf_op jit(solution)/shard_map/all_to_all | solution.py:72
  178.6 6.5 %fusion.95 = bf16[1,4,64,768]{3,2,1,0:T(8,128)(2,1)} fusion(bf16[1,4,64,768]{3,2,1,0:T(8,128)(2,1)S(1)} %bitcast.91, bf16[1,4,64,768]{3,2,1,0:T(8,128)(2,1)S(1)} %copy-done.9, bf16[1,3,64,768]{3,2,1,0:T(8,128)(2,1)S(1)} %collective-permute-done.10, bf16[1,3,64,768]{3,2,1,0:T(8,128)(2,1)S(1)} %collective-permute-done.9, ...), kind=kLoop, calls=%fused_computation.201 | loop fusion | flops 30474240 | bytes 18435072 | tf_op jit(solution)/shard_map/convert_element_type | solution.py:321
  185.1 2.1 %all-to-all-done.4 = f32[32,16,128]{2,1,0:T(8,128)S(1)} async-done(((f32[32,16,128]{2,1,0:T(8,128)}), f32[32,16,128]{2,1,0:T(8,128)S(1)}, u32[]{:S(2)}, u32[]{:S(2)}) %all-to-all-start.4) | async-done | bytes 262176 | tf_op jit(solution)/shard_map/all_to_all | solution.py:72
  (238 shorter events, 17.8 us)
Async XLA Ops:
  1.8 30.1 %collective-permute-start = (bf16[1,3,64,768]{3,2,1,0:T(8,128)(2,1)S(1)}, bf16[1,3,64,768]{3,2,1,0:T(8,128)(2,1)S(1)}, u32[]{:S(2)}, u32[]{:S(2)}) collective-permute-start(bf16[1,3,64,768]{3,2,1,0:T(8,128)(2,1)S(1)} %get-tuple-element.141), channel_id=1, source_target_pairs={{0,1},{1,2},{2,3},{3,4},{4,5},{5,6},{6,7},{7,8},{8,9},{9,10},{10,1... | collective-permute-start | bytes 884744 | tf_op jit(solution)/shard_map/ppermute | solution.py:24
  6.7 25.3 %collective-permute-start.1 = (bf16[1,3,64,768]{3,2,1,0:T(8,128)(2,1)S(1)}, bf16[1,3,64,768]{3,2,1,0:T(8,128)(2,1)}, u32[]{:S(2)}, u32[]{:S(2)}) collective-permute-start(bf16[1,3,64,768]{3,2,1,0:T(8,128)(2,1)S(1)} %get-tuple-element.142), channel_id=1, source_target_pairs={{1,0},{2,1},{3,2},{4,3},{5,4},{6,5},{7,6},{8,7},{9,8},{10,9},{11,1... | collective-permute-start | bytes 884744 | tf_op jit(solution)/shard_map/ppermute | solution.py:25
  16.5 27.2 %all-to-all-start = ((bf16[16,24,384]{2,1,0:T(8,128)(2,1)}), bf16[16,24,384]{2,1,0:T(8,128)(2,1)}, u32[]{:S(2)}, u32[]{:S(2)}) async-start(bf16[16,24,384]{2,1,0:T(8,128)(2,1)} %broadcast_in_dim.10), calls=%async_computation | async-start | bytes 589824 | tf_op jit(solution)/shard_map/all_to_all | solution.py:105
  46.0 14.8 %all-to-all-start.1 = ((bf16[4,16,24,384]{3,2,1,0:T(8,128)(2,1)}), bf16[4,16,24,384]{3,2,1,0:T(8,128)(2,1)}, u32[]{:S(2)}, u32[]{:S(2)}) async-start(bf16[4,16,24,384]{3,2,1,0:T(8,128)(2,1)} %broadcast_in_dim.11), calls=%async_computation.1 | async-start | bytes 2359296 | tf_op jit(solution)/shard_map/all_to_all | solution.py:110
  58.2 21.6 %copy-start.55 = (f32[3072]{0:T(1024)S(1)}, f32[3072]{0:T(1024)}, u32[]{:S(2)}) copy-start(f32[3072]{0:T(1024)} %param.13) | copy-start | bytes 36868
  62.2 11.6 %collective-permute-start.4 = (bf16[768,384]{1,0:T(8,128)(2,1)S(1)}, bf16[768,384]{1,0:T(8,128)(2,1)}, u32[]{:S(2)}, u32[]{:S(2)}) collective-permute-start(bf16[768,384]{1,0:T(8,128)(2,1)S(1)} %get-tuple-element.136.e0), channel_id=1, source_target_pairs={{0,64},{64,0},{128,192},{192,128},{1,65},{65,1},{129,193},{193,129... | collective-permute-start | bytes 1769480 | tf_op jit(solution)/shard_map/ppermute | solution.py:114
  65.3 12.5 %collective-permute-start.3 = (bf16[768,384]{1,0:T(8,128)(2,1)S(1)}, bf16[768,384]{1,0:T(8,128)(2,1)S(1)}, u32[]{:S(2)}, u32[]{:S(2)}) collective-permute-start(bf16[768,384]{1,0:T(8,128)(2,1)S(1)} %get-tuple-element.135.r0), channel_id=1, source_target_pairs={{0,192},{192,0},{64,128},{128,64},{1,193},{193,1},{65,129},{129,65... | collective-permute-start | bytes 1769480 | tf_op jit(solution)/shard_map/ppermute | solution.py:115
  69.0 31.0 %collective-permute-start.7 = (bf16[768,384]{1,0:T(8,128)(2,1)S(1)}, bf16[768,384]{1,0:T(8,128)(2,1)}, u32[]{:S(2)}, u32[]{:S(2)}) collective-permute-start(bf16[768,384]{1,0:T(8,128)(2,1)S(1)} %get-tuple-element.135.r0), channel_id=1, source_target_pairs={{0,64},{64,0},{128,192},{192,128},{1,65},{65,1},{129,193},{193,129... | collective-permute-start | bytes 1769480 | tf_op jit(solution)/shard_map/ppermute | solution.py:116
  71.3 33.4 %collective-permute-start.2 = (bf16[768,384]{1,0:T(8,128)(2,1)S(1)}, bf16[768,384]{1,0:T(8,128)(2,1)}, u32[]{:S(2)}, u32[]{:S(2)}) collective-permute-start(bf16[768,384]{1,0:T(8,128)(2,1)S(1)} %get-tuple-element.136.e0), channel_id=1, source_target_pairs={{0,192},{192,0},{64,128},{128,64},{1,193},{193,1},{65,129},{129,65... | collective-permute-start | bytes 1769480 | tf_op jit(solution)/shard_map/ppermute | solution.py:117
  73.8 30.8 %collective-permute-start.5 = (bf16[768,384]{1,0:T(8,128)(2,1)}, bf16[768,384]{1,0:T(8,128)(2,1)}, u32[]{:S(2)}, u32[]{:S(2)}) collective-permute-start(bf16[768,384]{1,0:T(8,128)(2,1)} %collective-permute-done.4.e1), channel_id=1, source_target_pairs={{0,192},{192,0},{64,128},{128,64},{1,193},{193,1},{65,129},{129,65... | collective-permute-start | bytes 1769480 | tf_op jit(solution)/shard_map/ppermute | solution.py:118
  77.8 26.8 %collective-permute-start.6 = (bf16[768,384]{1,0:T(8,128)(2,1)S(1)}, bf16[768,384]{1,0:T(8,128)(2,1)}, u32[]{:S(2)}, u32[]{:S(2)}) collective-permute-start(bf16[768,384]{1,0:T(8,128)(2,1)S(1)} %collective-permute-done.3.r0), channel_id=1, source_target_pairs={{0,64},{64,0},{128,192},{192,128},{1,65},{65,1},{129,193},{193,129... | collective-permute-start | bytes 1769480 | tf_op jit(solution)/shard_map/ppermute | solution.py:119
  111.3 8.9 %collective-permute-start.8 = (f32[256,768]{1,0:T(8,128)}, f32[256,768]{1,0:T(8,128)S(1)}, u32[]{:S(2)}, u32[]{:S(2)}) collective-permute-start(f32[256,768]{1,0:T(8,128)} %get-tuple-element.20), channel_id=1, source_target_pairs={{0,1},{1,0},{2,3},{3,2},{4,5},{5,4},{6,7},{7,6},{8,9},{9,8},{10,11... | collective-permute-start | bytes 2359304 | tf_op jit(solution)/shard_map/ppermute | solution.py:245
  141.4 28.9 %all-to-all-start.3 = ((f32[16,16,128]{2,1,0:T(8,128)}), f32[16,16,128]{2,1,0:T(8,128)S(1)}, u32[]{:S(2)}, u32[]{:S(2)}) async-start(f32[16,16,128]{2,1,0:T(8,128)} %broadcast_in_dim.13), calls=%async_computation.3 | async-start | bytes 262144 | tf_op jit(solution)/shard_map/all_to_all | solution.py:66
  158.0 20.4 %copy-start.9 = (bf16[1,4,64,768]{3,2,1,0:T(8,128)(2,1)S(1)}, bf16[1,4,64,768]{3,2,1,0:T(8,128)(2,1)}, u32[]{:S(2)}) copy-start(bf16[1,4,64,768]{3,2,1,0:T(8,128)(2,1)} %param.9) | copy-start | bytes 1179652
  158.0 20.4 %copy-start.12 = (f32[768]{0:T(1024)S(1)}, f32[768]{0:T(1024)}, u32[]{:S(2)}) copy-start(f32[768]{0:T(1024)} %get-tuple-element.110) | copy-start | bytes 9220
  158.0 20.4 %copy-start.14 = (f32[768]{0:T(1024)S(1)}, f32[768]{0:T(1024)}, u32[]{:S(2)}) copy-start(f32[768]{0:T(1024)} %get-tuple-element.111) | copy-start | bytes 9220
  158.1 20.4 %copy-start.16 = (f32[768]{0:T(1024)S(1)}, f32[768]{0:T(1024)}, u32[]{:S(2)}) copy-start(f32[768]{0:T(1024)} %get-tuple-element.112) | copy-start | bytes 9220
  158.1 20.4 %copy-start.18 = (f32[768]{0:T(1024)S(1)}, f32[768]{0:T(1024)}, u32[]{:S(2)}) copy-start(f32[768]{0:T(1024)} %get-tuple-element.113) | copy-start | bytes 9220
  158.1 20.4 %copy-start.20 = (f32[768]{0:T(1024)S(1)}, f32[768]{0:T(1024)}, u32[]{:S(2)}) copy-start(f32[768]{0:T(1024)} %get-tuple-element.114) | copy-start | bytes 9220
  158.1 20.4 %copy-start.22 = (f32[768]{0:T(1024)S(1)}, f32[768]{0:T(1024)}, u32[]{:S(2)}) copy-start(f32[768]{0:T(1024)} %get-tuple-element.115) | copy-start | bytes 9220
  158.1 20.4 %copy-start.24 = (f32[768]{0:T(1024)S(1)}, f32[768]{0:T(1024)}, u32[]{:S(2)}) copy-start(f32[768]{0:T(1024)} %get-tuple-element.116) | copy-start | bytes 9220
  158.1 20.4 %copy-start.26 = (f32[768]{0:T(1024)S(1)}, f32[768]{0:T(1024)}, u32[]{:S(2)}) copy-start(f32[768]{0:T(1024)} %get-tuple-element.117) | copy-start | bytes 9220
  158.1 20.4 %copy-start.28 = (f32[768]{0:T(1024)S(1)}, f32[768]{0:T(1024)}, u32[]{:S(2)}) copy-start(f32[768]{0:T(1024)} %get-tuple-element.118) | copy-start | bytes 9220
  158.1 20.4 %copy-start.30 = (f32[768]{0:T(1024)S(1)}, f32[768]{0:T(1024)}, u32[]{:S(2)}) copy-start(f32[768]{0:T(1024)} %get-tuple-element.119) | copy-start | bytes 9220
  158.1 20.4 %copy-start.32 = (f32[768]{0:T(1024)S(1)}, f32[768]{0:T(1024)}, u32[]{:S(2)}) copy-start(f32[768]{0:T(1024)} %get-tuple-element.120) | copy-start | bytes 9220
  158.1 20.4 %copy-start.34 = (f32[768]{0:T(1024)S(1)}, f32[768]{0:T(1024)}, u32[]{:S(2)}) copy-start(f32[768]{0:T(1024)} %get-tuple-element.121) | copy-start | bytes 9220
  158.2 20.4 %copy-start.36 = (f32[768]{0:T(1024)S(1)}, f32[768]{0:T(1024)}, u32[]{:S(2)}) copy-start(f32[768]{0:T(1024)} %get-tuple-element.122) | copy-start | bytes 9220
  158.2 20.4 %copy-start.38 = (f32[768]{0:T(1024)S(1)}, f32[768]{0:T(1024)}, u32[]{:S(2)}) copy-start(f32[768]{0:T(1024)} %get-tuple-element.123) | copy-start | bytes 9220
  158.2 20.4 %copy-start.40 = (f32[768]{0:T(1024)S(1)}, f32[768]{0:T(1024)}, u32[]{:S(2)}) copy-start(f32[768]{0:T(1024)} %get-tuple-element.124) | copy-start | bytes 9220
  158.3 11.8 %collective-permute-start.10 = (bf16[1,3,64,768]{3,2,1,0:T(8,128)(2,1)S(1)}, bf16[1,3,64,768]{3,2,1,0:T(8,128)(2,1)S(1)}, u32[]{:S(2)}, u32[]{:S(2)}) collective-permute-start(bf16[1,3,64,768]{3,2,1,0:T(8,128)(2,1)S(1)} %get-tuple-element.138), channel_id=1, source_target_pairs={{1,0},{2,1},{3,2},{4,3},{5,4},{6,5},{7,6},{8,7},{9,8},{10,9},{11,1... | collective-permute-start | bytes 884744 | tf_op jit(solution)/shard_map/ppermute | solution.py:25
  161.4 8.7 %collective-permute-start.9 = (bf16[1,3,64,768]{3,2,1,0:T(8,128)(2,1)S(1)}, bf16[1,3,64,768]{3,2,1,0:T(8,128)(2,1)S(1)}, u32[]{:S(2)}, u32[]{:S(2)}) collective-permute-start(bf16[1,3,64,768]{3,2,1,0:T(8,128)(2,1)S(1)} %get-tuple-element.137), channel_id=1, source_target_pairs={{0,1},{1,2},{2,3},{3,4},{4,5},{5,6},{6,7},{7,8},{8,9},{9,10},{10,1... | collective-permute-start | bytes 884744 | tf_op jit(solution)/shard_map/ppermute | solution.py:24
  171.1 16.1 %all-to-all-start.4 = ((f32[32,16,128]{2,1,0:T(8,128)}), f32[32,16,128]{2,1,0:T(8,128)S(1)}, u32[]{:S(2)}, u32[]{:S(2)}) async-start(f32[32,16,128]{2,1,0:T(8,128)} %broadcast_in_dim.14), calls=%async_computation.4 | async-start | bytes 524288 | tf_op jit(solution)/shard_map/all_to_all | solution.py:72
  (41 other events, 379.9 us)
